TPU v7x, 256 devices: a whole 4x4x8 slice. The times are simulated.
256 devices in a mesh: seq: 32 (over z, y), ffn: 8 (over x, core).
Axes of the slice: x: 4, y: 4, z: 8, core: 2. Of those that a mesh axis runs over, the one named last changes fastest.
Arguments:
- patches: bfloat16 [8192, 4096], P('seq'), may hold values from -100 to 100
- gate_weight: bfloat16 [4096, 7168], P('seq', 'ffn'), may hold values from -0.09375 to 0.09375
- up_weight: bfloat16 [4096, 7168], P('seq', 'ffn'), may hold values from -0.09375 to 0.09375
- down_weight: bfloat16 [4096, 7168], P('seq', 'ffn'), may hold values from -0.25 to 0.25
- key_weight: bfloat16 [4096, 1024], P(None, 'ffn'), may hold values from -0.09375 to 0.09375
- value_weight: bfloat16 [4096, 1024], P(None, 'ffn'), may hold values from -0.09375 to 0.09375
- byte_states: bfloat16 [65536, 1024], P('seq'), may hold values from -60 to 60
- byte_patch: int32 [65536], P('seq'), may hold values from 0 to 8191, as said below
- cross_query: bfloat16 [1024, 1024], P(None, 'ffn'), may hold values from -0.375 to 0.375
- self_query: bfloat16 [1024, 1024], P(None, 'ffn'), may hold values from -0.375 to 0.375
- self_key: bfloat16 [1024, 1024], P(None, 'ffn'), may hold values from -0.375 to 0.375
- self_value: bfloat16 [1024, 1024], P(None, 'ffn'), may hold values from -0.1875 to 0.1875
- cross_out: bfloat16 [1024, 1024], P('ffn'), may hold values from -0.1875 to 0.1875
- self_out: bfloat16 [1024, 1024], P('ffn'), may hold values from -0.1875 to 0.1875
Outputs:
- update: bfloat16 [65536, 1024], P('seq', 'ffn')
Inputs may be any that keep to these rules, and one draw needn't show every extreme that they name: byte_patch starts at 0, never falls, rises by at most 1 from one byte to the next and ends at 8191, so every patch is a run of one or more bytes. The bytes s * 2048 to (s + 1) * 2048 - 1 read only patches s * 256 - 23 to (s + 1) * 256 + 15; both ends are reached in every draw.
All inputs are finite; a program needn't handle non-finite values.
Results may differ from a plain program's by a relative error of at most 0.0085.
The roundings to bfloat16 on the way count: a program that leaves them out, or rounds other values in their place, can miss the bound.
Values may be sent and summed in bfloat16 or wider, within the bound.
No kernel may reach another device: no remote copies, remote signals or barrier semaphores. Data moves between devices by JAX's collectives and lax.ppermute only.
A program may use at most 128 MiB of HBM per device.

v0:
```python
import functools
import math

import jax
import jax.numpy as jnp
from jax import lax
from jax.experimental import pallas as pl
from jax.experimental.pallas import tpu as pltpu
from jax.sharding import Mesh, PartitionSpec as P


HD = 64
PWIN = 8
WINDOW = 512
HALO = 32
EPS = 1e-05
QROWS = 256
BROWS = 512

NZ, NY, NX, NC = 8, 4, 4, 2
NF = NX * NC
SEQ = ("z", "y")
FFN = ("x", "c")
BF = jnp.bfloat16
F32 = jnp.float32

UP = [(i, (i + 1) % 4) for i in range(4)]
DOWN = [(i, (i - 1) % 4) for i in range(4)]
ACROSS = [(i, (i + 2) % 4) for i in range(4)]
SCALE = 1.0 / math.sqrt(HD)


def sds(shape, dtype):
    return jax.ShapeDtypeStruct(shape, dtype)


def smem(*scalars):
    return jnp.stack([s.astype(jnp.int32) for s in scalars])


def cost(micros):
    return pl.CostEstimate(
        flops=int(micros * 6e8), transcendentals=0, bytes_accessed=int(micros * 2.5e6)
    )


def call(kernel, out, *args, micros=4, scalars=None, anywhere=(), scratch=()):
    offset = 0 if scalars is None else 1
    specs = [
        pl.BlockSpec(memory_space=pl.ANY if i in anywhere else pltpu.VMEM)
        for i in range(len(args))
    ]
    if offset:
        specs = [pl.BlockSpec(memory_space=pltpu.SMEM)] + specs
        args = (scalars,) + args
    return pl.pallas_call(
        kernel,
        out_shape=out,
        in_specs=specs,
        out_specs=jax.tree.map(lambda _: pl.BlockSpec(memory_space=pltpu.VMEM), out),
        scratch_shapes=list(scratch),
        cost_estimate=cost(micros),
    )(*args)


def swap(value, axes):
    return lax.all_to_all(value, axes, split_axis=0, concat_axis=0, tiled=True)


def ring(value, axis):
    half = value.shape[0] // 2
    before = lax.ppermute(value, axis, UP)
    after = lax.ppermute(value, axis, DOWN)
    far_low = lax.ppermute(before[:half], axis, UP)
    far_high = lax.ppermute(after[half:], axis, DOWN)
    return before, after, far_low, far_high


def other_core(value):
    return lax.ppermute(value, "c", [(0, 1), (1, 0)])


def dot(a, b):
    return jnp.dot(a, b, preferred_element_type=F32)


def dot_nt(a, b):
    return lax.dot_general(a, b, (((1,), (1,)), ((), ())), preferred_element_type=F32)


def norm_kernel(place, patches, _after, normed, half):
    wide = patches[...].astype(F32)
    mean = jnp.mean(wide * wide, axis=-1, keepdims=True)
    normed[...] = (wide * lax.rsqrt(mean + EPS)).astype(BF)
    half[...] = normed[pl.ds(pl.multiple_of(place[2] * half.shape[0], half.shape[0]), half.shape[0])]


def mix_kernel(place, down_t, *refs):
    out = refs[-1]
    x, core = place[0], place[2]
    lhs = jnp.concatenate([down_t[z] for z in range(NZ)], axis=1)
    for side in range(2):
        own, before, after, low, high = refs[5 * side : 5 * side + 5]
        at = core if side == 0 else 1 - core
        half = low.shape[0]
        out[NC * x + at] = dot(lhs, own[...])
        out[NC * ((x + 3) % NX) + at] = dot(lhs, before[...])
        out[NC * ((x + 1) % NX) + at] = dot(lhs, after[...])
        out[NC * ((x + 2) % NX) + at] = dot(lhs[:, :half], low[...]) + dot(
            lhs[:, half:], high[...]
        )


def mix_sum_kernel(terms, cross_out, self_out, mix, outs):
    total = terms[0]
    for i in range(1, NY):
        total = total + terms[i]
    total = total.astype(BF)
    for z in range(NZ):
        mix[z] = total
    rows = cross_out.shape[0]
    outs[:rows] = cross_out[...]
    outs[rows:] = self_out[...]


def project_kernel(states, w_qs, w_qc, w_k, w_v, qs, qc, kv):
    first = dot(states[...], jnp.concatenate([w_qs[...], w_qc[...]], axis=1)).astype(BF)
    cols = qs.shape[1]
    qs[...] = first[:, :cols]
    qc[...] = first[:, cols:]
    kv[...] = dot(states[...], jnp.concatenate([w_k[...], w_v[...]], axis=1)).astype(BF)


def project(states, w_qs, w_qc, w_k, w_v):
    count, width = states.shape
    cols = w_qs.shape[1]
    weight = pl.BlockSpec((width, cols), lambda i: (0, 0))
    narrow = pl.BlockSpec((BROWS, cols), lambda i: (i, 0))
    return pl.pallas_call(
        project_kernel,
        out_shape=(sds((count, cols), BF), sds((count, cols), BF), sds((count, 2 * cols), BF)),
        grid=(count // BROWS,),
        in_specs=[pl.BlockSpec((BROWS, width), lambda i: (i, 0))] + [weight] * 4,
        out_specs=(narrow, narrow, pl.BlockSpec((BROWS, 2 * cols), lambda i: (i, 0))),
        cost_estimate=cost(6),
    )(states, w_qs, w_qc, w_k, w_v)


def window_kernel(base, place, query, kv, before, out, stacked):
    step = pl.program_id(0) + base
    cols = query.shape[1]

    @pl.when(step == base)
    def _():
        stacked[:WINDOW] = before[...]
        stacked[WINDOW:] = kv[...]

    count = kv.shape[0]
    first = WINDOW - place[3] * count - step * QROWS
    row = lax.broadcasted_iota(jnp.int32, (QROWS, QROWS), 0)
    col = lax.broadcasted_iota(jnp.int32, (QROWS, QROWS), 1)
    tiles = WINDOW // QROWS + 1
    start = pl.multiple_of(step * QROWS, QROWS)
    for head in range(cols // HD):
        lanes = slice(head * HD, (head + 1) * HD)
        q = query[:, lanes] * SCALE
        scores = []
        for t in range(tiles):
            keys = stacked[pl.ds(start + t * QROWS, QROWS), lanes]
            s = dot_nt(q, keys)
            if t == 0:
                s = jnp.where((col > row) & (col >= first), s, -jnp.inf)
            elif t < tiles - 1:
                s = jnp.where(col >= first - t * QROWS, s, -jnp.inf)
            else:
                s = jnp.where(col <= row, s, -jnp.inf)
            scores.append(s)
        s = jnp.concatenate(scores, axis=1)
        e = jnp.exp(s - jnp.max(s, axis=-1, keepdims=True))
        w = (e * (1.0 / jnp.sum(e, axis=-1, keepdims=True))).astype(BF)
        values = stacked[
            pl.ds(start, tiles * QROWS), cols + head * HD : cols + (head + 1) * HD
        ]
        out[:, lanes] = dot(w, values).astype(BF)


def window_attention(place, query, kv, before, part):
    count, cols = query.shape
    steps = count // QROWS // 2
    first = part * steps
    block = pl.BlockSpec((QROWS, cols), lambda i: (i, 0))
    return pl.pallas_call(
        functools.partial(window_kernel, first),
        out_shape=sds((count // 2, cols), BF),
        grid=(steps,),
        in_specs=[
            pl.BlockSpec(memory_space=pltpu.SMEM),
            pl.BlockSpec((QROWS, cols), lambda i: (i + first, 0)),
            pl.BlockSpec(kv.shape, lambda i: (0, 0)),
            pl.BlockSpec(before.shape, lambda i: (0, 0)),
        ],
        out_specs=block,
        scratch_shapes=[pltpu.VMEM((WINDOW + count, 2 * cols), BF)],
        cost_estimate=cost(7),
    )(place, query, kv, before)


def ffn_kernel(place, *refs):
    pieces, gate_up = refs[:9], refs[9]
    outs = refs[10:14]
    rows_buf, weight_buf, sems = refs[14:]
    core = place[2]
    rows = pieces[0].shape[0]
    half, quarter = rows // 2, rows // 4
    own, other = core * half, (1 - core) * half
    starts = [0]
    for slab in (1, 2):
        starts += [slab * rows + own, slab * rows + other]
    starts += [3 * rows + own, 3 * rows + own + quarter]
    starts += [3 * rows + other, 3 * rows + other + quarter]
    weight_copy = pltpu.make_async_copy(gate_up, weight_buf, sems.at[9])
    weight_copy.start()
    copies = []
    for i, piece in enumerate(pieces):
        size = piece.shape[0]
        at = pl.multiple_of(starts[i], quarter)
        copies.append(pltpu.make_async_copy(piece, rows_buf.at[pl.ds(at, size)], sems.at[i]))
        copies[-1].start()
    slot = outs[0].shape[1]
    weight_copy.wait()
    for slab, used in enumerate(((0,), (1, 2), (3, 4), (5, 6, 7, 8))):
        for i in used:
            copies[i].wait()
        sums = dot(rows_buf[slab * rows : (slab + 1) * rows], weight_buf[...])
        gate = sums[:, :slot]
        outs[slab][...] = (gate * (1.0 / (1.0 + jnp.exp(-gate))) * sums[:, slot:]).astype(BF)


def part_kernel(place, own, after, before, far, m_own, m_after, m_before, m_low, m_high, out, hid):
    y = place[1]
    hid[y] = own[...]
    hid[(y + 1) % NY] = after[...]
    hid[(y + 3) % NY] = before[...]
    hid[(y + 2) % NY] = far[...]
    keep = 2 * m_own.shape[2]
    low = m_low.shape[0]

    def product(get):
        total = None
        for block in range(NY):
            piece = jnp.concatenate([get(2 * block), get(2 * block + 1)], axis=0)
            term = dot(hid[block, :, :keep], piece)
            total = term if total is None else total + term
        return total.astype(BF)

    for p in range(2):
        out[2 * y + p] = product(lambda z: m_own[z, p])
        out[2 * ((y + 1) % NY) + p] = product(lambda z: m_after[z, p])
        out[2 * ((y + 3) % NY) + p] = product(lambda z: m_before[z, p])
        out[2 * ((y + 2) % NY) + p] = product(
            lambda z: m_low[z, p] if z < low else m_high[z - low, p]
        )


def keys_kernel(parts, own, kv, head, tail):
    total = own[...]
    for i in range(NF):
        total = total + parts[i].astype(F32)
    total = total.astype(BF)
    kv[...] = total
    head[...] = total[:HALO]
    tail[...] = total[-HALO:]


def cross_kernel(place, query, byte_patch, kv, before, after, out, stacked):
    step = pl.program_id(0)
    rows, both = kv.shape
    cols = both // 2

    @pl.when(step == 0)
    def _():
        stacked[:HALO] = before[...]
        stacked[HALO : HALO + rows] = kv[...]
        stacked[HALO + rows :] = after[...]

    total = rows + 2 * HALO
    shape = (total, query.shape[0])
    index = lax.broadcasted_iota(jnp.int32, shape, 0) + (place[3] * rows - HALO)
    held = byte_patch[...]
    mask = (index <= held) & (index > held - PWIN) & (index >= 0)
    for head in range(cols // HD):
        q = query[:, head * HD : (head + 1) * HD] * SCALE
        s = dot_nt(stacked[:, head * HD : (head + 1) * HD], q)
        s = jnp.where(mask, s, -jnp.inf)
        e = jnp.exp(s - jnp.max(s, axis=0, keepdims=True))
        w = (e * (1.0 / jnp.sum(e, axis=0, keepdims=True))).astype(BF)
        values = stacked[:, cols + head * HD : cols + (head + 1) * HD]
        context = lax.dot_general(
            values, w, (((0,), (0,)), ((), ())), preferred_element_type=F32
        )
        out[:, head * HD : (head + 1) * HD] = context.T.astype(BF)


def cross_attention(place, query, byte_patch, kv, before, after):
    count, cols = query.shape
    block = pl.BlockSpec((BROWS, cols), lambda i: (i, 0))

    def whole(value):
        return pl.BlockSpec(value.shape, lambda i: (0, 0))

    return pl.pallas_call(
        cross_kernel,
        out_shape=sds((count, cols), BF),
        grid=(count // BROWS,),
        in_specs=[
            pl.BlockSpec(memory_space=pltpu.SMEM),
            block,
            pl.BlockSpec((1, BROWS), lambda i: (0, i)),
            whole(kv),
            whole(before),
            whole(after),
        ],
        out_specs=block,
        scratch_shapes=[pltpu.VMEM((kv.shape[0] + 2 * HALO, 2 * cols), BF)],
        cost_estimate=cost(6),
    )(place, query, byte_patch.reshape(1, count), kv, before, after)


def out_product(context, outs, which):
    both = outs.shape[0] // NF
    half = both // 2
    weight = jnp.concatenate(
        [outs[f * both + which * half : f * both + (which + 1) * half] for f in range(NF)], axis=0
    )
    return dot(jnp.concatenate([context[f] for f in range(NF)], axis=1), weight)


def self_part_kernel(context, outs, out):
    out[...] = out_product(context, outs, 1)


def update_kernel(context, outs, self_part, out):
    total = (self_part[...] + out_product(context, outs, 0)).astype(BF)
    cols = out.shape[2]
    for f in range(NF):
        out[f] = total[:, f * cols : (f + 1) * cols]


def local(
    patches,
    gate_weight,
    up_weight,
    down_weight,
    key_weight,
    value_weight,
    byte_states,
    byte_patch,
    cross_query,
    self_query,
    self_key,
    self_value,
    cross_out,
    self_out,
):
    x, y, core = (lax.axis_index(a) for a in ("x", "y", "c"))
    place = smem(x, y, core, lax.axis_index(SEQ))
    rows, width = patches.shape
    d_rows, hid = gate_weight.shape
    hid_y = hid // NY
    hid_z = hid // NZ
    pad_y = -hid_y % 128
    slot = hid_y + pad_y
    head_cols = key_weight.shape[1]
    both_cols = 2 * head_cols
    byte_count = byte_states.shape[0]
    chunk = byte_count // NF

    def by_y(weight):
        pieces = weight.reshape(d_rows, NY, hid_y).transpose(1, 0, 2)
        return jnp.pad(pieces, ((0, 0), (0, 0), (0, pad_y)))

    gate_up = jnp.concatenate([by_y(gate_weight), by_y(up_weight)], axis=2)
    gate_up = swap(gate_up, "y")
    gate_up = gate_up.reshape(NY * d_rows, 2 * slot)

    def of_y(weight):
        grid = weight.reshape(NZ, NY, d_rows, head_cols)
        return lax.dynamic_slice_in_dim(grid, y, 1, axis=1)

    kv_rows = jnp.concatenate([of_y(key_weight), of_y(value_weight)], axis=3)
    kv_rows = kv_rows.reshape(NZ * d_rows, both_cols)
    kv_pieces = (kv_rows,) + ring(kv_rows, "x")
    kv_others = tuple(other_core(piece) for piece in kv_pieces)

    normed, own_half = call(
        norm_kernel,
        (sds((rows, width), BF), sds((rows // NC, width), BF)),
        patches,
        gate_up,
        scalars=place,
        anywhere=(1,),
    )
    gate_up = lax.all_gather(gate_up, "z", axis=0, tiled=True)
    down_t = swap(down_weight.T.reshape(NZ, hid_z, d_rows), "z")
    before, after, far_low, far_high = ring(own_half, "y")
    group = (
        normed,
        after,
        other_core(after),
        before,
        other_core(before),
        far_low,
        far_high,
        other_core(far_low),
        other_core(far_high),
    )

    mix = call(
        mix_kernel,
        sds((NF, hid_z, both_cols), F32),
        down_t,
        *kv_pieces,
        *kv_others,
        scalars=place,
    )
    mix = swap(mix.reshape(NY, NF // NY * hid_z, both_cols), "y")
    mix, outs = call(
        mix_sum_kernel,
        (
            sds((NZ, NF // NY * hid_z, both_cols), BF),
            sds((2 * head_cols, NF * head_cols), BF),
        ),
        mix,
        cross_out,
        self_out,
    )
    mix = swap(mix, "z").reshape(NZ, NF // NY, hid_z, both_cols)
    m_before, m_after, m_low, m_high = ring(mix, "y")
    outs = lax.all_gather(outs, FFN, axis=0, tiled=True)

    own_kv = dot(patches, key_weight), dot(patches, value_weight)
    own_kv = jnp.concatenate(own_kv, axis=1)

    query_s, query_c, both_s = project(byte_states, self_query, cross_query, self_key, self_value)
    steps = [(i, i + 1) for i in range(NZ * NY - 1)]
    back = [(j, i) for i, j in steps]
    tail = lax.ppermute(both_s[byte_count - WINDOW :], SEQ, steps)
    halves = []
    for half in range(2):
        halves.append(window_attention(place, query_s, both_s, tail, half))
    context_s = jnp.concatenate(halves).reshape(NF, chunk, head_cols)
    context_s = swap(context_s, FFN)
    self_part = call(self_part_kernel, sds((chunk, NF * head_cols), F32), context_s, outs)
    piece = sds((rows, slot), BF)
    h_own, h_after, h_before, h_far = call(
        ffn_kernel,
        (piece,) * 4,
        *group,
        gate_up,
        scalars=place,
        anywhere=range(10),
        scratch=(
            pltpu.VMEM((NY * rows, width), BF),
            pltpu.VMEM(gate_up.shape, BF),
            pltpu.SemaphoreType.DMA((10,)),
        ),
    )
    hid_after = lax.ppermute(h_before, "y", DOWN)
    hid_before = lax.ppermute(h_after, "y", UP)
    hid_far = lax.ppermute(h_far, "y", ACROSS)
    part = call(
        part_kernel,
        sds((NF, rows, both_cols), BF),
        h_own,
        hid_after,
        hid_before,
        hid_far,
        mix,
        m_after,
        m_before,
        m_low,
        m_high,
        scalars=place,
        scratch=(pltpu.VMEM((NY, rows, slot), BF),),
    )
    part = swap(part, FFN)
    both_c, head_rows, tail_rows = call(
        keys_kernel,
        (sds((rows, both_cols), BF),) + (sds((HALO, both_cols), BF),) * 2,
        part,
        own_kv,
    )
    context_c = cross_attention(
        place,
        query_c,
        byte_patch,
        both_c,
        lax.ppermute(tail_rows, SEQ, steps),
        lax.ppermute(head_rows, SEQ, back),
    )
    context_c = swap(context_c.reshape(NF, chunk, head_cols), FFN)
    update = call(
        update_kernel, sds((NF, chunk, head_cols), BF), context_c, outs, self_part
    )
    return swap(update, FFN).reshape(byte_count, head_cols)


def solution(mesh):
    fine = Mesh(mesh.devices.reshape(NZ, NY, NX, NC), SEQ + FFN)
    placed = (
        P(SEQ, None),
        P(SEQ, FFN),
        P(SEQ, FFN),
        P(SEQ, FFN),
        P(None, FFN),
        P(None, FFN),
        P(SEQ, None),
        P(SEQ),
        P(None, FFN),
        P(None, FFN),
        P(None, FFN),
        P(None, FFN),
        P(FFN, None),
        P(FFN, None),
    )
    return jax.shard_map(
        local, mesh=fine, in_specs=placed, out_specs=P(SEQ, FFN), check_vma=False
    )
```

profile of v0, /device:TPU:1, one launch (start us, length us, event | category | flops | bytes accessed | tf_op | source)
XLA Modules:
  0.0 291.1 jit_solution(527081019202375948)
XLA Ops:
  8.8 13.4 %all_to_all.40 = bf16[4,128,512]{1,2,0:T(8,128)(2,1)S(1)} all-to-all(bf16[4,128,512]{1,2,0:T(8,128)(2,1)S(1)} %fusion.2), channel_id=1, replica_groups=mesh['z'=8,'y'=4,'x'=4,'c'=2] {'y'}, dimensions={0} | all-to-all | bytes 1048576 | tf_op jit(solution)/shard_map/all_to_all | solution.py:67
  29.6 7.8 %collective-permute-done.11.refs_1_ = bf16[1024,256]{1,0:T(8,128)(2,1)S(1)} collective-permute-done((bf16[1024,256]{1,0:T(8,128)(2,1)S(1)}, bf16[1024,256]{1,0:T(8,128)(2,1)S(1)}, u32[]{:S(2)}, u32[]{:S(2)}) %collective-permute-start.11) | collective-permute-done | bytes 524320 | tf_op jit(solution)/shard_map/ppermute | solution.py:72
  44.2 8.2 %all-to-all-start.1 = ((bf16[8,112,128]{2,1,0:T(8,128)(2,1)}), bf16[8,112,128]{2,1,0:T(8,128)(2,1)S(1)}, u32[]{:S(2)}, u32[]{:S(2)}) async-start(bf16[8,112,128]{2,1,0:T(8,128)(2,1)} %bitcast.11), calls=%async_computation.1 | async-start | bytes 458752 | tf_op jit(solution)/shard_map/all_to_all | solution.py:67
  54.3 11.8 %all-to-all-done.1.down_t = bf16[8,112,128]{2,1,0:T(8,128)(2,1)S(1)} async-done(((bf16[8,112,128]{2,1,0:T(8,128)(2,1)}), bf16[8,112,128]{2,1,0:T(8,128)(2,1)S(1)}, u32[]{:S(2)}, u32[]{:S(2)}) %all-to-all-start.1) | async-done | bytes 229408 | tf_op jit(solution)/shard_map/all_to_all | solution.py:67
  72.0 16.3 %all_to_all.41.terms = f32[4,224,256]{2,1,0:T(8,128)} all-to-all(f32[4,224,256]{2,1,0:T(8,128)} %bitcast.35), channel_id=1, replica_groups=mesh['z'=8,'y'=4,'x'=4,'c'=2] {'y'}, dimensions={0} | all-to-all | bytes 1835008 | tf_op jit(solution)/shard_map/all_to_all | solution.py:67
  90.9 4.2 %all-to-all-start.3 = ((bf16[8,224,256]{2,1,0:T(8,128)(2,1)}), bf16[8,224,256]{2,1,0:T(8,128)(2,1)}, u32[]{:S(2)}, u32[]{:S(2)}) async-start(bf16[8,224,256]{2,1,0:T(8,128)(2,1)} %get-tuple-element.26), calls=%async_computation.3 | async-start | bytes 1835008 | tf_op jit(solution)/shard_map/all_to_all | solution.py:67
  95.1 4.2 %shard_map.137 = (bf16[256,4096]{1,0:T(8,128)(2,1)}, bf16[128,4096]{1,0:T(8,128)(2,1)}) custom-call(s32[4]{0:T(128)} %pad_add_fusion.place, bf16[256,4096]{1,0:T(8,128)(2,1)} %patches.1, bf16[512,512]{1,0:T(8,128)(2,1)} %bitcast.31), custom_call_target="tpu_custom_call" | custom-call | flops 2400000000 | bytes 10000000 | tf_op jit(solution)/shard_map/pallas_call | solution.py:56
  102.0 17.5 %all-to-all-done.3 = bf16[8,224,256]{2,1,0:T(8,128)(2,1)} async-done(((bf16[8,224,256]{2,1,0:T(8,128)(2,1)}), bf16[8,224,256]{2,1,0:T(8,128)(2,1)}, u32[]{:S(2)}, u32[]{:S(2)}) %all-to-all-start.3) | async-done | bytes 917536 | tf_op jit(solution)/shard_map/all_to_all | solution.py:67
  126.8 6.4 %collective-permute-start.1 = (bf16[128,4096]{1,0:T(8,128)(2,1)}, bf16[128,4096]{1,0:T(8,128)(2,1)}, u32[]{:S(2)}, u32[]{:S(2)}) collective-permute-start(bf16[128,4096]{1,0:T(8,128)(2,1)} %collective-permute-done.refs_1_), channel_id=1, source_target_pairs={{0,1},{1,0},{2,3},{3,2},{4,5},{5,4},{6,7},{7,6},{8,9},{9,8},{10,11... | collective-permute-start | bytes 3145736 | tf_op jit(solution)/shard_map/ppermute | solution.py:80
  133.2 21.4 %collective-permute-done.4.refs_5_ = bf16[64,4096]{1,0:T(8,128)(2,1)} collective-permute-done((bf16[64,4096]{1,0:T(8,128)(2,1)S(1)}, bf16[64,4096]{1,0:T(8,128)(2,1)}, u32[]{:S(2)}, u32[]{:S(2)}) %collective-permute-start.4) | collective-permute-done | bytes 524320 | tf_op jit(solution)/shard_map/ppermute | solution.py:74
  160.2 6.0 %shard_map.136 = (bf16[2048,128]{1,0:T(8,128)(2,1)}, bf16[2048,128]{1,0:T(8,128)(2,1)}, bf16[2048,256]{1,0:T(8,128)(2,1)}) custom-call(bf16[2048,1024]{1,0:T(8,128)(2,1)} %states.1, bf16[1024,128]{1,0:T(8,128)(2,1)} %w_qs.1, bf16[1024,128]{1,0:T(8,128)(2,1)} %w_qc.1, bf16[1024,128]{1,0:T(8,128)(2,1)} %w_k.1, bf16[1024,128]{1,0:T(8,128)(2,1)} %w_v.1), custom_call_target="tpu_custom_call" | custom-call | flops 3600000000 | bytes 15000000 | tf_op jit(solution)/shard_map/pallas_call | solution.py:139
  168.0 6.2 %collective-permute-done.20.m_after = bf16[8,2,112,256]{3,2,1,0:T(8,128)(2,1)} collective-permute-done((bf16[8,2,112,256]{3,2,1,0:T(8,128)(2,1)}, bf16[8,2,112,256]{3,2,1,0:T(8,128)(2,1)}, u32[]{:S(2)}, u32[]{:S(2)}) %collective-permute-start.20) | collective-permute-done | bytes 917536 | tf_op jit(solution)/shard_map/ppermute | solution.py:73
  178.8 9.5 %shard_map.138 = (bf16[256,256]{1,0:T(8,128)(2,1)}, bf16[256,256]{1,0:T(8,128)(2,1)}, bf16[256,256]{1,0:T(8,128)(2,1)}, bf16[256,256]{1,0:T(8,128)(2,1)}) custom-call(s32[4]{0:T(128)} %pad_add_fusion.place, bf16[256,4096]{1,0:T(8,128)(2,1)} %get-tuple-element.20.refs_0_, bf16[128,4096]{1,0:T(8,128)(2,1)} %collective-permute-done.refs_1_, ...), custom_call_target="tpu_custom_call" | custom-call | flops 2400000000 | bytes 10000000 | tf_op jit(solution)/shard_map/pallas_call | solution.py:56
  196.9 4.5 %shard_map.141 = bf16[8,256,256]{2,1,0:T(8,128)(2,1)} custom-call(s32[4]{0:T(128)} %pad_add_fusion.place, bf16[256,256]{1,0:T(8,128)(2,1)} %get-tuple-element.22.own, bf16[256,256]{1,0:T(8,128)(2,1)} %copy-done.18, bf16[256,256]{1,0:T(8,128)(2,1)} %copy-done.19, bf16[256,256]{1,0:T(8,128)(2,1)} %collective-permute-done.10.far, ...), custom_call_target="tpu_custom_call" | custom-call | flops 2400000000 | bytes 10000000 | tf_op jit(solution)/shard_map/pallas_call | solution.py:56
  201.4 9.2 %all-to-all-start.4 = ((bf16[8,256,256]{2,1,0:T(8,128)(2,1)}), bf16[8,256,256]{2,1,0:T(8,128)(2,1)S(1)}, u32[]{:S(2)}, u32[]{:S(2)}) async-start(bf16[8,256,256]{2,1,0:T(8,128)(2,1)} %shard_map.141), calls=%async_computation.4 | async-start | bytes 2097152 | tf_op jit(solution)/shard_map/all_to_all | solution.py:67
  211.3 7.5 %shard_map.145 = bf16[1024,128]{1,0:T(8,128)(2,1)} custom-call(s32[4]{0:T(128)} %pad_add_fusion.place, bf16[2048,128]{1,0:T(8,128)(2,1)} %get-tuple-element.31.query, bf16[2048,256]{1,0:T(8,128)(2,1)} %get-tuple-element.32.kv, bf16[512,256]{1,0:T(8,128)(2,1)} %copy-done.17), custom_call_target="tpu_custom_call" | custom-call | flops 4200000000 | bytes 17500000 | tf_op jit(solution)/shard_map/pallas_call | solution.py:192
  218.8 7.5 %shard_map.144 = bf16[1024,128]{1,0:T(8,128)(2,1)} custom-call(s32[4]{0:T(128)} %pad_add_fusion.place, bf16[2048,128]{1,0:T(8,128)(2,1)} %get-tuple-element.31.query, bf16[2048,256]{1,0:T(8,128)(2,1)} %get-tuple-element.32.kv, bf16[512,256]{1,0:T(8,128)(2,1)} %copy-done.17), custom_call_target="tpu_custom_call" | custom-call | flops 4200000000 | bytes 17500000 | tf_op jit(solution)/shard_map/pallas_call | solution.py:192
  228.0 4.8 %all-to-all-start.6 = ((bf16[8,256,128]{2,1,0:T(8,128)(2,1)}), bf16[8,256,128]{2,1,0:T(8,128)(2,1)S(1)}, u32[]{:S(2)}, u32[]{:S(2)}) async-start(bf16[8,256,128]{2,1,0:T(8,128)(2,1)} %bitcast.18), calls=%async_computation.6 | async-start | bytes 1048576 | tf_op jit(solution)/shard_map/all_to_all | solution.py:67
  242.5 7.0 %shard_map.143 = bf16[2048,128]{1,0:T(8,128)(2,1)} custom-call(s32[4]{0:T(128)} %pad_add_fusion.place, bf16[2048,128]{1,0:T(8,128)(2,1)} %get-tuple-element.19.query, s32[1,2048]{1,0:T(1,128)} %bitcast.44, bf16[256,256]{1,0:T(8,128)(2,1)} %get-tuple-element.27.kv, bf16[32,256]{1,0:T(8,128)(2,1)} %copy-done.20, bf16[32,256]{1,0:T(8,128)(2,1)} %copy-done.21), custom_call_target="tpu_custom_call" | custom-call | flops 3600000000 | bytes 15000000 | tf_op jit(solution)/shard_map/pallas_call | solution.py:311
  249.6 5.9 %all-to-all-start.5 = ((bf16[8,256,128]{2,1,0:T(8,128)(2,1)}), bf16[8,256,128]{2,1,0:T(8,128)(2,1)S(1)}, u32[]{:S(2)}, u32[]{:S(2)}) async-start(bf16[8,256,128]{2,1,0:T(8,128)(2,1)} %bitcast.42), calls=%async_computation.5 | async-start | bytes 1048576 | tf_op jit(solution)/shard_map/all_to_all | solution.py:67
  255.4 4.1 %shard_map.146.self_part = f32[256,1024]{1,0:T(8,128)} custom-call(bf16[8,256,128]{2,1,0:T(8,128)(2,1)} %copy-done.5, bf16[2048,1024]{1,0:T(8,128)(2,1)} %all-gather.5.cloned.1.call-done.outs), custom_call_target="tpu_custom_call" | custom-call | flops 2400000000 | bytes 10000000 | tf_op jit(solution)/shard_map/pallas_call | solution.py:56
  259.5 5.3 %all-to-all-done.5.context = bf16[8,256,128]{2,1,0:T(8,128)(2,1)S(1)} async-done(((bf16[8,256,128]{2,1,0:T(8,128)(2,1)}), bf16[8,256,128]{2,1,0:T(8,128)(2,1)S(1)}, u32[]{:S(2)}, u32[]{:S(2)}) %all-to-all-start.5) | async-done | bytes 524320 | tf_op jit(solution)/shard_map/all_to_all | solution.py:67
  265.6 4.2 %shard_map.147 = bf16[8,256,128]{2,1,0:T(8,128)(2,1)} custom-call(bf16[8,256,128]{2,1,0:T(8,128)(2,1)} %copy-done.6, bf16[2048,1024]{1,0:T(8,128)(2,1)} %all-gather.5.cloned.1.call-done.outs, f32[256,1024]{1,0:T(8,128)} %shard_map.146.self_part), custom_call_target="tpu_custom_call" | custom-call | flops 2400000000 | bytes 10000000 | tf_op jit(solution)/shard_map/pallas_call | solution.py:56
  269.7 13.7 %all_to_all.42 = bf16[8,256,128]{2,1,0:T(8,128)(2,1)S(1)} all-to-all(bf16[8,256,128]{2,1,0:T(8,128)(2,1)} %shard_map.147), channel_id=1, replica_groups=mesh['z'=8,'y'=4,'x'=4,'c'=2] {'x','c'}, dimensions={0} | all-to-all | bytes 1048576 | tf_op jit(solution)/shard_map/all_to_all | solution.py:67
  (125 shorter events, 70.8 us)
Async XLA Ops:
  6.5 172.2 %all-gather.3.cloned.1.call-start = ((), (), s32[]{:S(2)}) async-start(), calls=%async_computation.8 | async-start | bytes 4718592 | tf_op jit(solution)/shard_map/all_gather | solution.py:403
  27.3 38.9 %collective-permute-start.15 = (bf16[1024,256]{1,0:T(8,128)(2,1)S(1)}, bf16[1024,256]{1,0:T(8,128)(2,1)S(1)}, u32[]{:S(2)}, u32[]{:S(2)}) collective-permute-start(bf16[1024,256]{1,0:T(8,128)(2,1)S(1)} %bitcast.40), channel_id=1, source_target_pairs={{0,1},{1,0},{2,3},{3,2},{4,5},{5,4},{6,7},{7,6},{8,9},{9,8},{10,11... | collective-permute-start | bytes 1572872 | tf_op jit(solution)/shard_map/ppermute | solution.py:80
  37.5 15.0 %collective-permute-start.13 = (bf16[512,256]{1,0:T(8,128)(2,1)S(1)}, bf16[512,256]{1,0:T(8,128)(2,1)}, u32[]{:S(2)}, u32[]{:S(2)}) collective-permute-start(bf16[512,256]{1,0:T(8,128)(2,1)S(1)} %slice.30), channel_id=1, source_target_pairs={{0,2},{2,4},{4,6},{6,0},{1,3},{3,5},{5,7},{7,1},{8,10},{10,12},{12... | collective-permute-start | bytes 786440 | tf_op jit(solution)/shard_map/ppermute | solution.py:74
  37.6 28.6 %collective-permute-start.16 = (bf16[1024,256]{1,0:T(8,128)(2,1)S(1)}, bf16[1024,256]{1,0:T(8,128)(2,1)S(1)}, u32[]{:S(2)}, u32[]{:S(2)}) collective-permute-start(bf16[1024,256]{1,0:T(8,128)(2,1)S(1)} %collective-permute-done.11.refs_1_), channel_id=1, source_target_pairs={{0,1},{1,0},{2,3},{3,2},{4,5},{5,4},{6,7},{7,6},{8,9},{9,8},{10,11... | collective-permute-start | bytes 1572872 | tf_op jit(solution)/shard_map/ppermute | solution.py:80
  40.5 25.6 %collective-permute-start.17 = (bf16[1024,256]{1,0:T(8,128)(2,1)S(1)}, bf16[1024,256]{1,0:T(8,128)(2,1)}, u32[]{:S(2)}, u32[]{:S(2)}) collective-permute-start(bf16[1024,256]{1,0:T(8,128)(2,1)S(1)} %collective-permute-done.12.refs_2_), channel_id=1, source_target_pairs={{0,1},{1,0},{2,3},{3,2},{4,5},{5,4},{6,7},{7,6},{8,9},{9,8},{10,11... | collective-permute-start | bytes 1572872 | tf_op jit(solution)/shard_map/ppermute | solution.py:80
  44.2 21.9 %all-to-all-start.1 = ((bf16[8,112,128]{2,1,0:T(8,128)(2,1)}), bf16[8,112,128]{2,1,0:T(8,128)(2,1)S(1)}, u32[]{:S(2)}, u32[]{:S(2)}) async-start(bf16[8,112,128]{2,1,0:T(8,128)(2,1)} %bitcast.11), calls=%async_computation.1 | async-start | bytes 458752 | tf_op jit(solution)/shard_map/all_to_all | solution.py:67
  52.4 203.0 %all-gather.5.cloned.1.call-start = ((), (), s32[]{:S(2)}) async-start(), calls=%async_computation.9 | async-start | bytes 4718592 | tf_op jit(solution)/shard_map/all_gather | solution.py:439
  90.9 28.6 %all-to-all-start.3 = ((bf16[8,224,256]{2,1,0:T(8,128)(2,1)}), bf16[8,224,256]{2,1,0:T(8,128)(2,1)}, u32[]{:S(2)}, u32[]{:S(2)}) async-start(bf16[8,224,256]{2,1,0:T(8,128)(2,1)} %get-tuple-element.26), calls=%async_computation.3 | async-start | bytes 1835008 | tf_op jit(solution)/shard_map/all_to_all | solution.py:67
  99.3 23.4 %collective-permute-start.2 = (bf16[128,4096]{1,0:T(8,128)(2,1)}, bf16[128,4096]{1,0:T(8,128)(2,1)S(1)}, u32[]{:S(2)}, u32[]{:S(2)}) collective-permute-start(bf16[128,4096]{1,0:T(8,128)(2,1)} %get-tuple-element.21), channel_id=1, source_target_pairs={{0,8},{8,16},{16,24},{24,0},{1,9},{9,17},{17,25},{25,1},{2,10},{10... | collective-permute-start | bytes 3145736 | tf_op jit(solution)/shard_map/ppermute | solution.py:72
  99.6 23.4 %collective-permute-start = (bf16[128,4096]{1,0:T(8,128)(2,1)}, bf16[128,4096]{1,0:T(8,128)(2,1)}, u32[]{:S(2)}, u32[]{:S(2)}) collective-permute-start(bf16[128,4096]{1,0:T(8,128)(2,1)} %get-tuple-element.21), channel_id=1, source_target_pairs={{0,24},{8,0},{16,8},{24,16},{1,25},{9,1},{17,9},{25,17},{2,26},{10... | collective-permute-start | bytes 3145736 | tf_op jit(solution)/shard_map/ppermute | solution.py:73
  119.5 37.8 %collective-permute-start.21 = (bf16[8,2,112,256]{3,2,1,0:T(8,128)(2,1)}, bf16[8,2,112,256]{3,2,1,0:T(8,128)(2,1)S(1)}, u32[]{:S(2)}, u32[]{:S(2)}) collective-permute-start(bf16[8,2,112,256]{3,2,1,0:T(8,128)(2,1)} %bitcast.16.m_own), channel_id=1, source_target_pairs={{0,8},{8,16},{16,24},{24,0},{1,9},{9,17},{17,25},{25,1},{2,10},{10... | collective-permute-start | bytes 2752520 | tf_op jit(solution)/shard_map/ppermute | solution.py:72
  122.7 31.9 %collective-permute-start.4 = (bf16[64,4096]{1,0:T(8,128)(2,1)S(1)}, bf16[64,4096]{1,0:T(8,128)(2,1)}, u32[]{:S(2)}, u32[]{:S(2)}) collective-permute-start(bf16[64,4096]{1,0:T(8,128)(2,1)S(1)} %slice.28), channel_id=1, source_target_pairs={{0,8},{8,16},{16,24},{24,0},{1,9},{9,17},{17,25},{25,1},{2,10},{10... | collective-permute-start | bytes 1572872 | tf_op jit(solution)/shard_map/ppermute | solution.py:74
  124.1 30.5 %collective-permute-start.5 = (bf16[64,4096]{1,0:T(8,128)(2,1)S(1)}, bf16[64,4096]{1,0:T(8,128)(2,1)}, u32[]{:S(2)}, u32[]{:S(2)}) collective-permute-start(bf16[64,4096]{1,0:T(8,128)(2,1)S(1)} %slice.29), channel_id=1, source_target_pairs={{0,24},{8,0},{16,8},{24,16},{1,25},{9,1},{17,9},{25,17},{2,26},{10... | collective-permute-start | bytes 1572872 | tf_op jit(solution)/shard_map/ppermute | solution.py:75
  126.8 49.2 %collective-permute-start.1 = (bf16[128,4096]{1,0:T(8,128)(2,1)}, bf16[128,4096]{1,0:T(8,128)(2,1)}, u32[]{:S(2)}, u32[]{:S(2)}) collective-permute-start(bf16[128,4096]{1,0:T(8,128)(2,1)} %collective-permute-done.refs_1_), channel_id=1, source_target_pairs={{0,1},{1,0},{2,3},{3,2},{4,5},{5,4},{6,7},{7,6},{8,9},{9,8},{10,11... | collective-permute-start | bytes 3145736 | tf_op jit(solution)/shard_map/ppermute | solution.py:80
  133.2 45.5 %collective-permute-start.3 = (bf16[128,4096]{1,0:T(8,128)(2,1)S(1)}, bf16[128,4096]{1,0:T(8,128)(2,1)}, u32[]{:S(2)}, u32[]{:S(2)}) collective-permute-start(bf16[128,4096]{1,0:T(8,128)(2,1)S(1)} %collective-permute-done.2.refs_3_), channel_id=1, source_target_pairs={{0,1},{1,0},{2,3},{3,2},{4,5},{5,4},{6,7},{7,6},{8,9},{9,8},{10,11... | collective-permute-start | bytes 3145736 | tf_op jit(solution)/shard_map/ppermute | solution.py:80
  154.6 19.6 %collective-permute-start.20 = (bf16[8,2,112,256]{3,2,1,0:T(8,128)(2,1)}, bf16[8,2,112,256]{3,2,1,0:T(8,128)(2,1)}, u32[]{:S(2)}, u32[]{:S(2)}) collective-permute-start(bf16[8,2,112,256]{3,2,1,0:T(8,128)(2,1)} %bitcast.16.m_own), channel_id=1, source_target_pairs={{0,24},{8,0},{16,8},{24,16},{1,25},{9,1},{17,9},{25,17},{2,26},{10... | collective-permute-start | bytes 2752520 | tf_op jit(solution)/shard_map/ppermute | solution.py:73
  154.6 24.1 %collective-permute-start.6 = (bf16[64,4096]{1,0:T(8,128)(2,1)}, bf16[64,4096]{1,0:T(8,128)(2,1)}, u32[]{:S(2)}, u32[]{:S(2)}) collective-permute-start(bf16[64,4096]{1,0:T(8,128)(2,1)} %collective-permute-done.4.refs_5_), channel_id=1, source_target_pairs={{0,1},{1,0},{2,3},{3,2},{4,5},{5,4},{6,7},{7,6},{8,9},{9,8},{10,11... | collective-permute-start | bytes 1572872 | tf_op jit(solution)/shard_map/ppermute | solution.py:80
  158.2 20.5 %collective-permute-start.7 = (bf16[64,4096]{1,0:T(8,128)(2,1)}, bf16[64,4096]{1,0:T(8,128)(2,1)}, u32[]{:S(2)}, u32[]{:S(2)}) collective-permute-start(bf16[64,4096]{1,0:T(8,128)(2,1)} %collective-permute-done.5.refs_6_), channel_id=1, source_target_pairs={{0,1},{1,0},{2,3},{3,2},{4,5},{5,4},{6,7},{7,6},{8,9},{9,8},{10,11... | collective-permute-start | bytes 1572872 | tf_op jit(solution)/shard_map/ppermute | solution.py:80
  174.2 17.4 %collective-permute-start.22 = (bf16[4,2,112,256]{3,2,1,0:T(8,128)(2,1)}, bf16[4,2,112,256]{3,2,1,0:T(8,128)(2,1)}, u32[]{:S(2)}, u32[]{:S(2)}) collective-permute-start(bf16[4,2,112,256]{3,2,1,0:T(8,128)(2,1)} %slice.32), channel_id=1, source_target_pairs={{0,8},{8,16},{16,24},{24,0},{1,9},{9,17},{17,25},{25,1},{2,10},{10... | collective-permute-start | bytes 1376264 | tf_op jit(solution)/shard_map/ppermute | solution.py:74
  176.1 20.2 %collective-permute-start.23 = (bf16[4,2,112,256]{3,2,1,0:T(8,128)(2,1)}, bf16[4,2,112,256]{3,2,1,0:T(8,128)(2,1)}, u32[]{:S(2)}, u32[]{:S(2)}) collective-permute-start(bf16[4,2,112,256]{3,2,1,0:T(8,128)(2,1)} %slice.33), channel_id=1, source_target_pairs={{0,24},{8,0},{16,8},{24,16},{1,25},{9,1},{17,9},{25,17},{2,26},{10... | collective-permute-start | bytes 1376264 | tf_op jit(solution)/shard_map/ppermute | solution.py:75
  191.6 19.0 %collective-permute-start.26 = (bf16[512,256]{1,0:T(8,128)(2,1)S(1)}, bf16[512,256]{1,0:T(8,128)(2,1)S(1)}, u32[]{:S(2)}, u32[]{:S(2)}) collective-permute-start(bf16[512,256]{1,0:T(8,128)(2,1)S(1)} %slice.27), channel_id=1, source_target_pairs={{0,8},{8,16},{16,24},{24,32},{32,40},{40,48},{48,56},{56,64},{64,7... | collective-permute-start | bytes 786440 | tf_op jit(solution)/shard_map/ppermute | solution.py:447
  201.4 26.6 %all-to-all-start.4 = ((bf16[8,256,256]{2,1,0:T(8,128)(2,1)}), bf16[8,256,256]{2,1,0:T(8,128)(2,1)S(1)}, u32[]{:S(2)}, u32[]{:S(2)}) async-start(bf16[8,256,256]{2,1,0:T(8,128)(2,1)} %shard_map.141), calls=%async_computation.4 | async-start | bytes 2097152 | tf_op jit(solution)/shard_map/all_to_all | solution.py:67
  228.0 21.5 %all-to-all-start.6 = ((bf16[8,256,128]{2,1,0:T(8,128)(2,1)}), bf16[8,256,128]{2,1,0:T(8,128)(2,1)S(1)}, u32[]{:S(2)}, u32[]{:S(2)}) async-start(bf16[8,256,128]{2,1,0:T(8,128)(2,1)} %bitcast.18), calls=%async_computation.6 | async-start | bytes 1048576 | tf_op jit(solution)/shard_map/all_to_all | solution.py:67
  249.6 15.2 %all-to-all-start.5 = ((bf16[8,256,128]{2,1,0:T(8,128)(2,1)}), bf16[8,256,128]{2,1,0:T(8,128)(2,1)S(1)}, u32[]{:S(2)}, u32[]{:S(2)}) async-start(bf16[8,256,128]{2,1,0:T(8,128)(2,1)} %bitcast.42), calls=%async_computation.5 | async-start | bytes 1048576 | tf_op jit(solution)/shard_map/all_to_all | solution.py:67
  (32 other events, 351.9 us)
Sparse Core Ops, SparseCore 0:
  23.4 61.5 all-gather.2
  91.0 29.6 all-gather.4
where the time goes:
time: 296 us; the launch traced here: 291 us
  waiting for transfers between devices  76.8 us (26%)
  starting transfers between devices  70.9 us (24%)
  Pallas kernels  62.9 us (21%)
  blocking collectives  43.4 us (15%)
  local copies, waits for them, and re-layouts  17.3 us (6%)
  between operations  13.8 us (5%)
  other arithmetic  3.28 us (1%)
    all_to_all x3, blocking collectives, swap(): return lax.all_to_all(value, axes, split_axis=0, concat_axis=0, tiled=True)  43.4 us
    pallas_call x8, Pallas kernels, call(): pl.pallas_call(kernel, out_shape=out, in_specs=specs, out_specs=jax.tree....  34.9 us
    all_to_all x5, waiting for transfers between devices, swap(): return lax.all_to_all(value, axes, split_axis=0, concat_axis=0, tiled=True)  34.6 us
    all_to_all x5, starting transfers between devices, swap(): return lax.all_to_all(value, axes, split_axis=0, concat_axis=0, tiled=True)  32.3 us
    ppermute x3, waiting for transfers between devices, ring(): far_low = lax.ppermute(before[:half], axis, UP)  21.4 us
    ppermute x9, starting transfers between devices, other_core(): return lax.ppermute(value, 'c', [(0, 1), (1, 0)])  15.6 us
    pallas_call x2, Pallas kernels, window_attention(): pl.pallas_call(functools.partial(window_kernel, first), out_shape=sds((co...  14.9 us
    ppermute x3, waiting for transfers between devices, ring(): before = lax.ppermute(value, axis, UP)  10.7 us
  transfers between devices with their start and end apart: 34, of which 8 were waited for; matrix products, arithmetic and copies ran while one was open for 5% of the time, Pallas kernels for 20%

commit v1 on v0

--- a/solution.py
+++ b/solution.py
@@ -67,8 +67,12 @@
     return lax.all_to_all(value, axes, split_axis=0, concat_axis=0, tiled=True)
 
 
+def spread(value, axes, count):
+    return swap(jnp.broadcast_to(value[None], (count,) + value.shape), axes)
+
+
 def ring(value, axis):
-    half = value.shape[0] // 2
+    half = -(-value.shape[0] // 32) * 16
     before = lax.ppermute(value, axis, UP)
     after = lax.ppermute(value, axis, DOWN)
     far_low = lax.ppermute(before[:half], axis, UP)
@@ -99,28 +103,27 @@
     out = refs[-1]
     x, core = place[0], place[2]
     lhs = jnp.concatenate([down_t[z] for z in range(NZ)], axis=1)
+    cols = refs[0].shape[1]
+
+    def store(at, value):
+        out[:, pl.ds(pl.multiple_of(at * cols, cols), cols)] = value.astype(BF)
+
     for side in range(2):
         own, before, after, low, high = refs[5 * side : 5 * side + 5]
         at = core if side == 0 else 1 - core
         half = low.shape[0]
-        out[NC * x + at] = dot(lhs, own[...])
-        out[NC * ((x + 3) % NX) + at] = dot(lhs, before[...])
-        out[NC * ((x + 1) % NX) + at] = dot(lhs, after[...])
-        out[NC * ((x + 2) % NX) + at] = dot(lhs[:, :half], low[...]) + dot(
-            lhs[:, half:], high[...]
-        )
-
-
-def mix_sum_kernel(terms, cross_out, self_out, mix, outs):
-    total = terms[0]
-    for i in range(1, NY):
-        total = total + terms[i]
-    total = total.astype(BF)
-    for z in range(NZ):
-        mix[z] = total
-    rows = cross_out.shape[0]
-    outs[:rows] = cross_out[...]
-    outs[rows:] = self_out[...]
+        store(NC * x + at, dot(lhs, own[...]))
+        store(NC * ((x + 3) % NX) + at, dot(lhs, before[...]))
+        store(NC * ((x + 1) % NX) + at, dot(lhs, after[...]))
+        far = dot(lhs[:, :half], low[...]) + dot(lhs[:, half:], high[...])
+        store(NC * ((x + 2) % NX) + at, far)
+
+
+def mix_sum_kernel(own, before, after, low, high, mix):
+    half = low.shape[0]
+    near = own[...].astype(F32) + before[...].astype(F32) + after[...].astype(F32)
+    mix[:half] = (near[:half] + low[...].astype(F32)).astype(BF)
+    mix[half:] = (near[half:] + high[...].astype(F32)).astype(BF)
 
 
 def project_kernel(states, w_qs, w_qc, w_k, w_v, qs, qc, kv):
@@ -236,54 +239,42 @@
         outs[slab][...] = (gate * (1.0 / (1.0 + jnp.exp(-gate))) * sums[:, slot:]).astype(BF)
 
 
-def part_kernel(place, own, after, before, far, m_own, m_after, m_before, m_low, m_high, out, hid):
+def edge_kernel(place, own, after, before, far, head, tail):
     y = place[1]
-    hid[y] = own[...]
-    hid[(y + 1) % NY] = after[...]
-    hid[(y + 3) % NY] = before[...]
-    hid[(y + 2) % NY] = far[...]
-    keep = 2 * m_own.shape[2]
-    low = m_low.shape[0]
-
-    def product(get):
+    for step, ref in enumerate((own, after, far, before)):
+        head[(y + step) % NY] = ref[:HALO]
+        tail[(y + step) % NY] = ref[-HALO:]
+
+
+def part_kernel(place, own, after, before, far, above, below, mix, out, hid):
+    y = place[1]
+    rows = own.shape[0]
+    for step, ref in enumerate((own, after, far, before)):
+        hid[(y + step) % NY, HALO : HALO + rows] = ref[...]
+    hid[:, :HALO] = above[...]
+    hid[:, HALO + rows :] = below[...]
+    keep = mix.shape[0] // NY
+    cols = out.shape[2]
+    for f in range(NF):
         total = None
         for block in range(NY):
-            piece = jnp.concatenate([get(2 * block), get(2 * block + 1)], axis=0)
+            piece = mix[block * keep : (block + 1) * keep, f * cols : (f + 1) * cols]
             term = dot(hid[block, :, :keep], piece)
             total = term if total is None else total + term
-        return total.astype(BF)
-
-    for p in range(2):
-        out[2 * y + p] = product(lambda z: m_own[z, p])
-        out[2 * ((y + 1) % NY) + p] = product(lambda z: m_after[z, p])
-        out[2 * ((y + 3) % NY) + p] = product(lambda z: m_before[z, p])
-        out[2 * ((y + 2) % NY) + p] = product(
-            lambda z: m_low[z, p] if z < low else m_high[z - low, p]
-        )
-
-
-def keys_kernel(parts, own, kv, head, tail):
-    total = own[...]
+        out[f] = total.astype(BF)
+
+
+def keys_kernel(parts, own, above, below, kv):
+    total = jnp.concatenate([above[...], own[...], below[...]], axis=0)
     for i in range(NF):
         total = total + parts[i].astype(F32)
-    total = total.astype(BF)
-    kv[...] = total
-    head[...] = total[:HALO]
-    tail[...] = total[-HALO:]
-
-
-def cross_kernel(place, query, byte_patch, kv, before, after, out, stacked):
-    step = pl.program_id(0)
-    rows, both = kv.shape
+    kv[...] = total.astype(BF)
+
+
+def cross_kernel(place, query, byte_patch, stacked, out):
+    total, both = stacked.shape
     cols = both // 2
-
-    @pl.when(step == 0)
-    def _():
-        stacked[:HALO] = before[...]
-        stacked[HALO : HALO + rows] = kv[...]
-        stacked[HALO + rows :] = after[...]
-
-    total = rows + 2 * HALO
+    rows = total - 2 * HALO
     shape = (total, query.shape[0])
     index = lax.broadcasted_iota(jnp.int32, shape, 0) + (place[3] * rows - HALO)
     held = byte_patch[...]
@@ -301,13 +292,9 @@
         out[:, head * HD : (head + 1) * HD] = context.T.astype(BF)
 
 
-def cross_attention(place, query, byte_patch, kv, before, after):
+def cross_attention(place, query, byte_patch, kv):
     count, cols = query.shape
     block = pl.BlockSpec((BROWS, cols), lambda i: (i, 0))
-
-    def whole(value):
-        return pl.BlockSpec(value.shape, lambda i: (0, 0))
-
     return pl.pallas_call(
         cross_kernel,
         out_shape=sds((count, cols), BF),
@@ -316,14 +303,11 @@
             pl.BlockSpec(memory_space=pltpu.SMEM),
             block,
             pl.BlockSpec((1, BROWS), lambda i: (0, i)),
-            whole(kv),
-            whole(before),
-            whole(after),
+            pl.BlockSpec(kv.shape, lambda i: (0, 0)),
         ],
         out_specs=block,
-        scratch_shapes=[pltpu.VMEM((kv.shape[0] + 2 * HALO, 2 * cols), BF)],
         cost_estimate=cost(6),
-    )(place, query, byte_patch.reshape(1, count), kv, before, after)
+    )(place, query, byte_patch.reshape(1, count), kv)
 
 
 def out_product(context, outs, which):
@@ -417,33 +401,26 @@
 
     mix = call(
         mix_kernel,
-        sds((NF, hid_z, both_cols), F32),
+        sds((hid_z, NF * both_cols), BF),
         down_t,
         *kv_pieces,
         *kv_others,
         scalars=place,
     )
-    mix = swap(mix.reshape(NY, NF // NY * hid_z, both_cols), "y")
-    mix, outs = call(
-        mix_sum_kernel,
-        (
-            sds((NZ, NF // NY * hid_z, both_cols), BF),
-            sds((2 * head_cols, NF * head_cols), BF),
-        ),
-        mix,
-        cross_out,
-        self_out,
-    )
-    mix = swap(mix, "z").reshape(NZ, NF // NY, hid_z, both_cols)
-    m_before, m_after, m_low, m_high = ring(mix, "y")
-    outs = lax.all_gather(outs, FFN, axis=0, tiled=True)
-
+    mixes = ring(mix, "y")
+    mix = call(mix_sum_kernel, sds(mix.shape, BF), mix, *mixes)
+    mix = lax.all_gather(mix, "z", axis=0, tiled=True)
+    outs = spread(jnp.concatenate([cross_out, self_out]), FFN, NF)
+    outs = outs.reshape(NF * 2 * head_cols, NF * head_cols)
+
+    steps = [(i, i + 1) for i in range(NZ * NY - 1)]
+    back = [(j, i) for i, j in steps]
     own_kv = dot(patches, key_weight), dot(patches, value_weight)
     own_kv = jnp.concatenate(own_kv, axis=1)
+    own_above = lax.ppermute(own_kv[-HALO:], SEQ, steps)
+    own_below = lax.ppermute(own_kv[:HALO], SEQ, back)
 
     query_s, query_c, both_s = project(byte_states, self_query, cross_query, self_key, self_value)
-    steps = [(i, i + 1) for i in range(NZ * NY - 1)]
-    back = [(j, i) for i, j in steps]
     tail = lax.ppermute(both_s[byte_count - WINDOW :], SEQ, steps)
     halves = []
     for half in range(2):
@@ -468,36 +445,36 @@
     hid_after = lax.ppermute(h_before, "y", DOWN)
     hid_before = lax.ppermute(h_after, "y", UP)
     hid_far = lax.ppermute(h_far, "y", ACROSS)
+    edges = (sds((NY, HALO, slot), BF),) * 2
+    head, tail = call(
+        edge_kernel, edges, h_own, hid_after, hid_before, hid_far, micros=2, scalars=place
+    )
+    above = lax.ppermute(tail, SEQ, steps)
+    below = lax.ppermute(head, SEQ, back)
     part = call(
         part_kernel,
-        sds((NF, rows, both_cols), BF),
+        sds((NF, rows + 2 * HALO, both_cols), BF),
         h_own,
         hid_after,
         hid_before,
         hid_far,
+        above,
+        below,
         mix,
-        m_after,
-        m_before,
-        m_low,
-        m_high,
         scalars=place,
-        scratch=(pltpu.VMEM((NY, rows, slot), BF),),
+        scratch=(pltpu.VMEM((NY, rows + 2 * HALO, slot), BF),),
     )
     part = swap(part, FFN)
-    both_c, head_rows, tail_rows = call(
+    both_c = call(
         keys_kernel,
-        (sds((rows, both_cols), BF),) + (sds((HALO, both_cols), BF),) * 2,
+        sds((rows + 2 * HALO, both_cols), BF),
         part,
         own_kv,
-    )
-    context_c = cross_attention(
-        place,
-        query_c,
-        byte_patch,
-        both_c,
-        lax.ppermute(tail_rows, SEQ, steps),
-        lax.ppermute(head_rows, SEQ, back),
-    )
+        own_above,
+        own_below,
+    )
+
+    context_c = cross_attention(place, query_c, byte_patch, both_c)
     context_c = swap(context_c.reshape(NF, chunk, head_cols), FFN)
     update = call(
         update_kernel, sds((NF, chunk, head_cols), BF), context_c, outs, self_part
@@ -523,6 +500,4 @@
         P(FFN, None),
         P(FFN, None),
     )
-    return jax.shard_map(
-        local, mesh=fine, in_specs=placed, out_specs=P(SEQ, FFN), check_vma=False
-    )
+    return jax.shard_map(local, mesh=fine, in_specs=placed, out_specs=P(SEQ, FFN), check_vma=False)

time: 296 us -> 322 us (1.088)
  waiting for transfers between devices: 76.8 us -> 113 us
  blocking collectives: 43.4 us -> 27.1 us
  starting transfers between devices: 70.9 us -> 76.1 us
    all_to_all x5, waiting for transfers between devices: 34.6 us -> 64.1 us  [swap(): return lax.all_to_all(value, axes, split_axis=0, concat_axis=0, tiled=True)]
    ppermute x3, waiting for transfers between devices: 10.7 us -> 37.5 us  [ring(): before = lax.ppermute(value, axis, UP)]
    ppermute x3, waiting for transfers between devices: 21.4 us -> 1.22 us  [ring(): far_low = lax.ppermute(before[:half], axis, UP)]
    all_to_all x3 -> x2, blocking collectives: 43.4 us -> 27.1 us  [swap(): return lax.all_to_all(value, axes, split_axis=0, concat_axis=0, tiled=True)]
    ppermute x3, waiting for transfers between devices: 6.2 us -> 0.01 us  [ring(): after = lax.ppermute(value, axis, DOWN)]
    ppermute x2 -> x4, starting transfers between devices: 3.23 us -> 8.64 us  [the longest x1 4.16 us: local(): above = lax.ppermute(tail, SEQ, steps)]
    ppermute x2 -> x4, waiting for transfers between devices: 3.75 us -> 7.79 us  [the longest x1 3.87 us: local(): own_below = lax.ppermute(own_kv[:HALO], SEQ, back)]
    ppermute x1, starting transfers between devices: 0.36 us -> 4.27 us  [local(): hid_after = lax.ppermute(h_before, 'y', DOWN)]
  transfers between devices with their start and end apart: 34 -> 36, of which waited for: 8 -> 12; matrix products, arithmetic and copies ran while one was open for 5% -> 3% of each run, Pallas kernels for 20% -> 19%
where the time goes in v1:
time: 322 us; the launch traced here: 319 us
  waiting for transfers between devices  113 us (35%)
  starting transfers between devices  76.1 us (24%)
  Pallas kernels  65 us (20%)
  blocking collectives  27.1 us (8%)
  local copies, waits for them, and re-layouts  19.5 us (6%)
  between operations  13.8 us (4%)
    all_to_all x5, waiting for transfers between devices, swap(): return lax.all_to_all(value, axes, split_axis=0, concat_axis=0, tiled=True)  64.1 us
    ppermute x3, waiting for transfers between devices, ring(): before = lax.ppermute(value, axis, UP)  37.5 us
    pallas_call x9, Pallas kernels, call(): pl.pallas_call(kernel, out_shape=out, in_specs=specs, out_specs=jax.tree....  37.1 us
    all_to_all x5, starting transfers between devices, swap(): return lax.all_to_all(value, axes, split_axis=0, concat_axis=0, tiled=True)  31.9 us
    all_to_all x2, blocking collectives, swap(): return lax.all_to_all(value, axes, split_axis=0, concat_axis=0, tiled=True)  27.1 us
    pallas_call x2, Pallas kernels, window_attention(): pl.pallas_call(functools.partial(window_kernel, first), out_shape=sds((co...  14.9 us
    unnamed x66, local copies, waits for them, and re-layouts  12.2 us
    ppermute x9, starting transfers between devices, other_core(): return lax.ppermute(value, 'c', [(0, 1), (1, 0)])  12.1 us
  transfers between devices with their start and end apart: 36, of which 12 were waited for; matrix products, arithmetic and copies ran while one was open for 3% of the time, Pallas kernels for 19%

profile of v1, /device:TPU:1, one launch (start us, length us, event | category | flops | bytes accessed | tf_op | source)
XLA Modules:
  0.0 318.6 jit_solution(12865697689616812598)
XLA Ops:
  8.9 13.4 %all_to_all.35 = bf16[4,128,512]{1,2,0:T(8,128)(2,1)S(1)} all-to-all(bf16[4,128,512]{1,2,0:T(8,128)(2,1)S(1)} %fusion.2), channel_id=1, replica_groups=mesh['z'=8,'y'=4,'x'=4,'c'=2] {'y'}, dimensions={0} | all-to-all | bytes 1048576 | tf_op jit(solution)/shard_map/all_to_all | solution.py:67
  29.7 7.8 %collective-permute-done.13.refs_1_ = bf16[1024,256]{1,0:T(8,128)(2,1)S(1)} collective-permute-done((bf16[1024,256]{1,0:T(8,128)(2,1)S(1)}, bf16[1024,256]{1,0:T(8,128)(2,1)S(1)}, u32[]{:S(2)}, u32[]{:S(2)}) %collective-permute-start.13) | collective-permute-done | bytes 524320 | tf_op jit(solution)/shard_map/ppermute | solution.py:76
  44.3 8.2 %all-to-all-start.1 = ((bf16[8,112,128]{2,1,0:T(8,128)(2,1)}), bf16[8,112,128]{2,1,0:T(8,128)(2,1)S(1)}, u32[]{:S(2)}, u32[]{:S(2)}) async-start(bf16[8,112,128]{2,1,0:T(8,128)(2,1)} %bitcast.11), calls=%async_computation.1 | async-start | bytes 458752 | tf_op jit(solution)/shard_map/all_to_all | solution.py:67
  54.3 11.9 %all-to-all-done.1.down_t = bf16[8,112,128]{2,1,0:T(8,128)(2,1)S(1)} async-done(((bf16[8,112,128]{2,1,0:T(8,128)(2,1)}), bf16[8,112,128]{2,1,0:T(8,128)(2,1)S(1)}, u32[]{:S(2)}, u32[]{:S(2)}) %all-to-all-start.1) | async-done | bytes 229408 | tf_op jit(solution)/shard_map/all_to_all | solution.py:67
  74.2 9.4 %collective-permute-done.22.before = bf16[112,2048]{1,0:T(8,128)(2,1)S(1)} collective-permute-done((bf16[112,2048]{1,0:T(8,128)(2,1)}, bf16[112,2048]{1,0:T(8,128)(2,1)S(1)}, u32[]{:S(2)}, u32[]{:S(2)}) %collective-permute-start.22) | collective-permute-done | bytes 458784 | tf_op jit(solution)/shard_map/ppermute | solution.py:76
  93.6 4.2 %shard_map.137 = (bf16[256,4096]{1,0:T(8,128)(2,1)}, bf16[128,4096]{1,0:T(8,128)(2,1)}) custom-call(s32[4]{0:T(128)} %pad_add_fusion.place, bf16[256,4096]{1,0:T(8,128)(2,1)} %patches.1, bf16[512,512]{1,0:T(8,128)(2,1)} %bitcast.30), custom_call_target="tpu_custom_call" | custom-call | flops 2400000000 | bytes 10000000 | tf_op jit(solution)/shard_map/pallas_call | solution.py:56
  100.5 20.2 %collective-permute-done.2.refs_3_ = bf16[128,4096]{1,0:T(8,128)(2,1)S(1)} collective-permute-done((bf16[128,4096]{1,0:T(8,128)(2,1)}, bf16[128,4096]{1,0:T(8,128)(2,1)S(1)}, u32[]{:S(2)}, u32[]{:S(2)}) %collective-permute-start.2) | collective-permute-done | bytes 1048608 | tf_op jit(solution)/shard_map/ppermute | solution.py:76
  125.2 6.0 %shard_map.136 = (bf16[2048,128]{1,0:T(8,128)(2,1)}, bf16[2048,128]{1,0:T(8,128)(2,1)}, bf16[2048,256]{1,0:T(8,128)(2,1)}) custom-call(bf16[2048,1024]{1,0:T(8,128)(2,1)} %states.1, bf16[1024,128]{1,0:T(8,128)(2,1)} %w_qs.1, bf16[1024,128]{1,0:T(8,128)(2,1)} %w_qc.1, bf16[1024,128]{1,0:T(8,128)(2,1)} %w_k.1, bf16[1024,128]{1,0:T(8,128)(2,1)} %w_v.1), custom_call_target="tpu_custom_call" | custom-call | flops 3600000000 | bytes 15000000 | tf_op jit(solution)/shard_map/pallas_call | solution.py:142
  133.5 4.7 %collective-permute-start.1 = (bf16[128,4096]{1,0:T(8,128)(2,1)S(1)}, bf16[128,4096]{1,0:T(8,128)(2,1)}, u32[]{:S(2)}, u32[]{:S(2)}) collective-permute-start(bf16[128,4096]{1,0:T(8,128)(2,1)S(1)} %collective-permute-done.refs_1_), channel_id=1, source_target_pairs={{0,1},{1,0},{2,3},{3,2},{4,5},{5,4},{6,7},{7,6},{8,9},{9,8},{10,11... | collective-permute-start | bytes 3145736 | tf_op jit(solution)/shard_map/ppermute | solution.py:84
  139.8 7.5 %shard_map.146 = bf16[1024,128]{1,0:T(8,128)(2,1)} custom-call(s32[4]{0:T(128)} %pad_add_fusion.place, bf16[2048,128]{1,0:T(8,128)(2,1)} %get-tuple-element.25.query, bf16[2048,256]{1,0:T(8,128)(2,1)} %get-tuple-element.26.kv, bf16[512,256]{1,0:T(8,128)(2,1)} %copy-done.21), custom_call_target="tpu_custom_call" | custom-call | flops 4200000000 | bytes 17500000 | tf_op jit(solution)/shard_map/pallas_call | solution.py:195
  147.3 7.4 %shard_map.145 = bf16[1024,128]{1,0:T(8,128)(2,1)} custom-call(s32[4]{0:T(128)} %pad_add_fusion.place, bf16[2048,128]{1,0:T(8,128)(2,1)} %get-tuple-element.25.query, bf16[2048,256]{1,0:T(8,128)(2,1)} %get-tuple-element.26.kv, bf16[512,256]{1,0:T(8,128)(2,1)} %copy-done.21), custom_call_target="tpu_custom_call" | custom-call | flops 4200000000 | bytes 17500000 | tf_op jit(solution)/shard_map/pallas_call | solution.py:195
  154.7 9.5 %shard_map.138 = (bf16[256,256]{1,0:T(8,128)(2,1)}, bf16[256,256]{1,0:T(8,128)(2,1)}, bf16[256,256]{1,0:T(8,128)(2,1)}, bf16[256,256]{1,0:T(8,128)(2,1)}) custom-call(s32[4]{0:T(128)} %pad_add_fusion.place, bf16[256,4096]{1,0:T(8,128)(2,1)} %get-tuple-element.17.refs_0_, bf16[128,4096]{1,0:T(8,128)(2,1)} %copy-done.2, ...), custom_call_target="tpu_custom_call" | custom-call | flops 2400000000 | bytes 10000000 | tf_op jit(solution)/shard_map/pallas_call | solution.py:56
  164.2 4.3 %collective-permute-start.8 = (bf16[256,256]{1,0:T(8,128)(2,1)}, bf16[256,256]{1,0:T(8,128)(2,1)S(1)}, u32[]{:S(2)}, u32[]{:S(2)}) collective-permute-start(bf16[256,256]{1,0:T(8,128)(2,1)} %get-tuple-element.20), channel_id=1, source_target_pairs={{0,24},{8,0},{16,8},{24,16},{1,25},{9,1},{17,9},{25,17},{2,26},{10... | collective-permute-start | bytes 393224 | tf_op jit(solution)/shard_map/ppermute | solution.py:445
  170.6 7.6 %all-to-all-start.5 = ((bf16[8,256,128]{2,1,0:T(8,128)(2,1)}), bf16[8,256,128]{2,1,0:T(8,128)(2,1)S(1)}, u32[]{:S(2)}, u32[]{:S(2)}) async-start(bf16[8,256,128]{2,1,0:T(8,128)(2,1)} %bitcast.17), calls=%async_computation.5 | async-start | bytes 1048576 | tf_op jit(solution)/shard_map/all_to_all | solution.py:67
  190.7 5.0 %shard_map.142 = bf16[8,320,256]{2,1,0:T(8,128)(2,1)} custom-call(s32[4]{0:T(128)} %pad_add_fusion.place, bf16[256,256]{1,0:T(8,128)(2,1)} %get-tuple-element.19.own, bf16[256,256]{1,0:T(8,128)(2,1)} %copy-done.24, bf16[256,256]{1,0:T(8,128)(2,1)} %copy-done.25, bf16[256,256]{1,0:T(8,128)(2,1)} %copy-done.26, bf16[4,32,256]{2,1,0:T(8,128)(2,1)} %copy-done.27, ...), custom_call_target="tpu_custom_call" | custom-call | flops 2400000000 | bytes 10000000 | tf_op jit(solution)/shard_map/pallas_call | solution.py:56
  196.5 6.2 %all-to-all-start.2 = ((bf16[8,320,256]{2,1,0:T(8,128)(2,1)}), bf16[8,320,256]{2,1,0:T(8,128)(2,1)S(1)}, u32[]{:S(2)}, u32[]{:S(2)}) async-start(bf16[8,320,256]{2,1,0:T(8,128)(2,1)} %shard_map.142), calls=%async_computation.2 | async-start | bytes 2621440 | tf_op jit(solution)/shard_map/all_to_all | solution.py:67
  202.8 17.7 %all-to-all-done.2.parts = bf16[8,320,256]{2,1,0:T(8,128)(2,1)S(1)} async-done(((bf16[8,320,256]{2,1,0:T(8,128)(2,1)}), bf16[8,320,256]{2,1,0:T(8,128)(2,1)S(1)}, u32[]{:S(2)}, u32[]{:S(2)}) %all-to-all-start.2) | async-done | bytes 1310752 | tf_op jit(solution)/shard_map/all_to_all | solution.py:67
  224.2 5.5 %all-to-all-start.4 = ((bf16[8,256,1024]{2,1,0:T(8,128)(2,1)}), bf16[8,256,1024]{2,1,0:T(8,128)(2,1)}, u32[]{:S(2)}, u32[]{:S(2)}) async-start(bf16[8,256,1024]{2,1,0:T(8,128)(2,1)} %broadcast_in_dim.2), calls=%async_computation.4 | async-start | bytes 8388608 | tf_op jit(solution)/shard_map/all_to_all | solution.py:67
  242.3 7.0 %shard_map.144 = bf16[2048,128]{1,0:T(8,128)(2,1)} custom-call(s32[4]{0:T(128)} %pad_add_fusion.place, bf16[2048,128]{1,0:T(8,128)(2,1)} %get-tuple-element.16.query, s32[1,2048]{1,0:T(1,128)} %bitcast.42, bf16[320,256]{1,0:T(8,128)(2,1)} %shard_map.143.stacked), custom_call_target="tpu_custom_call" | custom-call | flops 3600000000 | bytes 15000000 | tf_op jit(solution)/shard_map/pallas_call | solution.py:298
  249.3 29.2 %all-to-all-done.4 = bf16[8,256,1024]{2,1,0:T(8,128)(2,1)} async-done(((bf16[8,256,1024]{2,1,0:T(8,128)(2,1)}), bf16[8,256,1024]{2,1,0:T(8,128)(2,1)}, u32[]{:S(2)}, u32[]{:S(2)}) %all-to-all-start.4) | async-done | bytes 4194336 | tf_op jit(solution)/shard_map/all_to_all | solution.py:67
  278.6 4.4 %all-to-all-start.3 = ((bf16[8,256,128]{2,1,0:T(8,128)(2,1)}), bf16[8,256,128]{2,1,0:T(8,128)(2,1)S(1)}, u32[]{:S(2)}, u32[]{:S(2)}) async-start(bf16[8,256,128]{2,1,0:T(8,128)(2,1)} %bitcast.40), calls=%async_computation.3 | async-start | bytes 1048576 | tf_op jit(solution)/shard_map/all_to_all | solution.py:67
  287.0 5.3 %all-to-all-done.3.context = bf16[8,256,128]{2,1,0:T(8,128)(2,1)S(1)} async-done(((bf16[8,256,128]{2,1,0:T(8,128)(2,1)}), bf16[8,256,128]{2,1,0:T(8,128)(2,1)S(1)}, u32[]{:S(2)}, u32[]{:S(2)}) %all-to-all-start.3) | async-done | bytes 524320 | tf_op jit(solution)/shard_map/all_to_all | solution.py:67
  293.1 4.2 %shard_map.148 = bf16[8,256,128]{2,1,0:T(8,128)(2,1)} custom-call(bf16[8,256,128]{2,1,0:T(8,128)(2,1)} %copy-done.8, bf16[2048,1024]{1,0:T(8,128)(2,1)} %bitcast.16.outs, f32[256,1024]{1,0:T(8,128)} %shard_map.147.self_part), custom_call_target="tpu_custom_call" | custom-call | flops 2400000000 | bytes 10000000 | tf_op jit(solution)/shard_map/pallas_call | solution.py:56
  297.3 13.7 %all_to_all.36 = bf16[8,256,128]{2,1,0:T(8,128)(2,1)S(1)} all-to-all(bf16[8,256,128]{2,1,0:T(8,128)(2,1)} %shard_map.148), channel_id=1, replica_groups=mesh['z'=8,'y'=4,'x'=4,'c'=2] {'x','c'}, dimensions={0} | all-to-all | bytes 1048576 | tf_op jit(solution)/shard_map/all_to_all | solution.py:67
  (150 shorter events, 84.4 us)
Async XLA Ops:
  6.5 148.2 %all-gather.3.cloned.1.call-start = ((), (), s32[]{:S(2)}) async-start(), calls=%async_computation.7 | async-start | bytes 4718592 | tf_op jit(solution)/shard_map/all_gather | solution.py:387
  24.5 13.0 %collective-permute-start.13 = (bf16[1024,256]{1,0:T(8,128)(2,1)S(1)}, bf16[1024,256]{1,0:T(8,128)(2,1)S(1)}, u32[]{:S(2)}, u32[]{:S(2)}) collective-permute-start(bf16[1024,256]{1,0:T(8,128)(2,1)S(1)} %bitcast.36), channel_id=1, source_target_pairs={{0,2},{2,4},{4,6},{6,0},{1,3},{3,5},{5,7},{7,1},{8,10},{10,12},{12... | collective-permute-start | bytes 1572872 | tf_op jit(solution)/shard_map/ppermute | solution.py:76
  25.8 14.7 %collective-permute-start.14 = (bf16[1024,256]{1,0:T(8,128)(2,1)S(1)}, bf16[1024,256]{1,0:T(8,128)(2,1)S(1)}, u32[]{:S(2)}, u32[]{:S(2)}) collective-permute-start(bf16[1024,256]{1,0:T(8,128)(2,1)S(1)} %bitcast.37), channel_id=1, source_target_pairs={{0,6},{2,0},{4,2},{6,4},{1,7},{3,1},{5,3},{7,5},{8,14},{10,8},{12,... | collective-permute-start | bytes 1572872 | tf_op jit(solution)/shard_map/ppermute | solution.py:77
  27.3 38.9 %collective-permute-start.17 = (bf16[1024,256]{1,0:T(8,128)(2,1)S(1)}, bf16[1024,256]{1,0:T(8,128)(2,1)}, u32[]{:S(2)}, u32[]{:S(2)}) collective-permute-start(bf16[1024,256]{1,0:T(8,128)(2,1)S(1)} %bitcast.38), channel_id=1, source_target_pairs={{0,1},{1,0},{2,3},{3,2},{4,5},{5,4},{6,7},{7,6},{8,9},{9,8},{10,11... | collective-permute-start | bytes 1572872 | tf_op jit(solution)/shard_map/ppermute | solution.py:84
  37.5 15.0 %collective-permute-start.15 = (bf16[512,256]{1,0:T(8,128)(2,1)S(1)}, bf16[512,256]{1,0:T(8,128)(2,1)}, u32[]{:S(2)}, u32[]{:S(2)}) collective-permute-start(bf16[512,256]{1,0:T(8,128)(2,1)S(1)} %slice.38), channel_id=1, source_target_pairs={{0,2},{2,4},{4,6},{6,0},{1,3},{3,5},{5,7},{7,1},{8,10},{10,12},{12... | collective-permute-start | bytes 786440 | tf_op jit(solution)/shard_map/ppermute | solution.py:78
  37.6 28.6 %collective-permute-start.18 = (bf16[1024,256]{1,0:T(8,128)(2,1)S(1)}, bf16[1024,256]{1,0:T(8,128)(2,1)}, u32[]{:S(2)}, u32[]{:S(2)}) collective-permute-start(bf16[1024,256]{1,0:T(8,128)(2,1)S(1)} %collective-permute-done.13.refs_1_), channel_id=1, source_target_pairs={{0,1},{1,0},{2,3},{3,2},{4,5},{5,4},{6,7},{7,6},{8,9},{9,8},{10,11... | collective-permute-start | bytes 1572872 | tf_op jit(solution)/shard_map/ppermute | solution.py:84
  40.6 25.6 %collective-permute-start.19 = (bf16[1024,256]{1,0:T(8,128)(2,1)S(1)}, bf16[1024,256]{1,0:T(8,128)(2,1)}, u32[]{:S(2)}, u32[]{:S(2)}) collective-permute-start(bf16[1024,256]{1,0:T(8,128)(2,1)S(1)} %collective-permute-done.14.refs_2_), channel_id=1, source_target_pairs={{0,1},{1,0},{2,3},{3,2},{4,5},{5,4},{6,7},{7,6},{8,9},{9,8},{10,11... | collective-permute-start | bytes 1572872 | tf_op jit(solution)/shard_map/ppermute | solution.py:84
  40.7 12.9 %collective-permute-start.16 = (bf16[512,256]{1,0:T(8,128)(2,1)S(1)}, bf16[512,256]{1,0:T(8,128)(2,1)}, u32[]{:S(2)}, u32[]{:S(2)}) collective-permute-start(bf16[512,256]{1,0:T(8,128)(2,1)S(1)} %slice.39), channel_id=1, source_target_pairs={{0,6},{2,0},{4,2},{6,4},{1,7},{3,1},{5,3},{7,5},{8,14},{10,8},{12,... | collective-permute-start | bytes 786440 | tf_op jit(solution)/shard_map/ppermute | solution.py:79
  44.3 21.9 %all-to-all-start.1 = ((bf16[8,112,128]{2,1,0:T(8,128)(2,1)}), bf16[8,112,128]{2,1,0:T(8,128)(2,1)S(1)}, u32[]{:S(2)}, u32[]{:S(2)}) async-start(bf16[8,112,128]{2,1,0:T(8,128)(2,1)} %bitcast.11), calls=%async_computation.1 | async-start | bytes 458752 | tf_op jit(solution)/shard_map/all_to_all | solution.py:67
  52.5 137.7 %all-gather.5.cloned.1.call-start = ((), (), s32[]{:S(2)}) async-start(), calls=%async_computation.8 | async-start | bytes 4128768 | tf_op jit(solution)/shard_map/all_gather | solution.py:412
  52.5 13.7 %collective-permute-start.20 = (bf16[512,256]{1,0:T(8,128)(2,1)}, bf16[512,256]{1,0:T(8,128)(2,1)S(1)}, u32[]{:S(2)}, u32[]{:S(2)}) collective-permute-start(bf16[512,256]{1,0:T(8,128)(2,1)} %collective-permute-done.15.refs_3_), channel_id=1, source_target_pairs={{0,1},{1,0},{2,3},{3,2},{4,5},{5,4},{6,7},{7,6},{8,9},{9,8},{10,11... | collective-permute-start | bytes 786440 | tf_op jit(solution)/shard_map/ppermute | solution.py:84
  97.8 22.9 %collective-permute-start.2 = (bf16[128,4096]{1,0:T(8,128)(2,1)}, bf16[128,4096]{1,0:T(8,128)(2,1)S(1)}, u32[]{:S(2)}, u32[]{:S(2)}) collective-permute-start(bf16[128,4096]{1,0:T(8,128)(2,1)} %get-tuple-element.18), channel_id=1, source_target_pairs={{0,8},{8,16},{16,24},{24,0},{1,9},{9,17},{17,25},{25,1},{2,10},{10... | collective-permute-start | bytes 3145736 | tf_op jit(solution)/shard_map/ppermute | solution.py:76
  97.8 23.8 %collective-permute-start = (bf16[128,4096]{1,0:T(8,128)(2,1)}, bf16[128,4096]{1,0:T(8,128)(2,1)S(1)}, u32[]{:S(2)}, u32[]{:S(2)}) collective-permute-start(bf16[128,4096]{1,0:T(8,128)(2,1)} %get-tuple-element.18), channel_id=1, source_target_pairs={{0,24},{8,0},{16,8},{24,16},{1,25},{9,1},{17,9},{25,17},{2,26},{10... | collective-permute-start | bytes 3145736 | tf_op jit(solution)/shard_map/ppermute | solution.py:77
  121.6 16.8 %collective-permute-start.4 = (bf16[64,4096]{1,0:T(8,128)(2,1)}, bf16[64,4096]{1,0:T(8,128)(2,1)}, u32[]{:S(2)}, u32[]{:S(2)}) collective-permute-start(bf16[64,4096]{1,0:T(8,128)(2,1)} %slice.36), channel_id=1, source_target_pairs={{0,8},{8,16},{16,24},{24,0},{1,9},{9,17},{17,25},{25,1},{2,10},{10... | collective-permute-start | bytes 1572872 | tf_op jit(solution)/shard_map/ppermute | solution.py:78
  122.5 16.2 %collective-permute-start.5 = (bf16[64,4096]{1,0:T(8,128)(2,1)}, bf16[64,4096]{1,0:T(8,128)(2,1)}, u32[]{:S(2)}, u32[]{:S(2)}) collective-permute-start(bf16[64,4096]{1,0:T(8,128)(2,1)} %slice.37), channel_id=1, source_target_pairs={{0,24},{8,0},{16,8},{24,16},{1,25},{9,1},{17,9},{25,17},{2,26},{10... | collective-permute-start | bytes 1572872 | tf_op jit(solution)/shard_map/ppermute | solution.py:79
  133.5 21.1 %collective-permute-start.1 = (bf16[128,4096]{1,0:T(8,128)(2,1)S(1)}, bf16[128,4096]{1,0:T(8,128)(2,1)}, u32[]{:S(2)}, u32[]{:S(2)}) collective-permute-start(bf16[128,4096]{1,0:T(8,128)(2,1)S(1)} %collective-permute-done.refs_1_), channel_id=1, source_target_pairs={{0,1},{1,0},{2,3},{3,2},{4,5},{5,4},{6,7},{7,6},{8,9},{9,8},{10,11... | collective-permute-start | bytes 3145736 | tf_op jit(solution)/shard_map/ppermute | solution.py:84
  138.2 16.4 %collective-permute-start.3 = (bf16[128,4096]{1,0:T(8,128)(2,1)S(1)}, bf16[128,4096]{1,0:T(8,128)(2,1)}, u32[]{:S(2)}, u32[]{:S(2)}) collective-permute-start(bf16[128,4096]{1,0:T(8,128)(2,1)S(1)} %collective-permute-done.2.refs_3_), channel_id=1, source_target_pairs={{0,1},{1,0},{2,3},{3,2},{4,5},{5,4},{6,7},{7,6},{8,9},{9,8},{10,11... | collective-permute-start | bytes 3145736 | tf_op jit(solution)/shard_map/ppermute | solution.py:84
  138.4 16.3 %collective-permute-start.6 = (bf16[64,4096]{1,0:T(8,128)(2,1)}, bf16[64,4096]{1,0:T(8,128)(2,1)}, u32[]{:S(2)}, u32[]{:S(2)}) collective-permute-start(bf16[64,4096]{1,0:T(8,128)(2,1)} %collective-permute-done.4.refs_5_), channel_id=1, source_target_pairs={{0,1},{1,0},{2,3},{3,2},{4,5},{5,4},{6,7},{7,6},{8,9},{9,8},{10,11... | collective-permute-start | bytes 1572872 | tf_op jit(solution)/shard_map/ppermute | solution.py:84
  138.8 15.9 %collective-permute-start.7 = (bf16[64,4096]{1,0:T(8,128)(2,1)}, bf16[64,4096]{1,0:T(8,128)(2,1)}, u32[]{:S(2)}, u32[]{:S(2)}) collective-permute-start(bf16[64,4096]{1,0:T(8,128)(2,1)} %collective-permute-done.5.refs_6_), channel_id=1, source_target_pairs={{0,1},{1,0},{2,3},{3,2},{4,5},{5,4},{6,7},{7,6},{8,9},{9,8},{10,11... | collective-permute-start | bytes 1572872 | tf_op jit(solution)/shard_map/ppermute | solution.py:84
  164.2 13.9 %collective-permute-start.8 = (bf16[256,256]{1,0:T(8,128)(2,1)}, bf16[256,256]{1,0:T(8,128)(2,1)S(1)}, u32[]{:S(2)}, u32[]{:S(2)}) collective-permute-start(bf16[256,256]{1,0:T(8,128)(2,1)} %get-tuple-element.20), channel_id=1, source_target_pairs={{0,24},{8,0},{16,8},{24,16},{1,25},{9,1},{17,9},{25,17},{2,26},{10... | collective-permute-start | bytes 393224 | tf_op jit(solution)/shard_map/ppermute | solution.py:445
  170.6 25.1 %all-to-all-start.5 = ((bf16[8,256,128]{2,1,0:T(8,128)(2,1)}), bf16[8,256,128]{2,1,0:T(8,128)(2,1)S(1)}, u32[]{:S(2)}, u32[]{:S(2)}) async-start(bf16[8,256,128]{2,1,0:T(8,128)(2,1)} %bitcast.17), calls=%async_computation.5 | async-start | bytes 1048576 | tf_op jit(solution)/shard_map/all_to_all | solution.py:67
  196.5 24.0 %all-to-all-start.2 = ((bf16[8,320,256]{2,1,0:T(8,128)(2,1)}), bf16[8,320,256]{2,1,0:T(8,128)(2,1)S(1)}, u32[]{:S(2)}, u32[]{:S(2)}) async-start(bf16[8,320,256]{2,1,0:T(8,128)(2,1)} %shard_map.142), calls=%async_computation.2 | async-start | bytes 2621440 | tf_op jit(solution)/shard_map/all_to_all | solution.py:67
  224.2 54.4 %all-to-all-start.4 = ((bf16[8,256,1024]{2,1,0:T(8,128)(2,1)}), bf16[8,256,1024]{2,1,0:T(8,128)(2,1)}, u32[]{:S(2)}, u32[]{:S(2)}) async-start(bf16[8,256,1024]{2,1,0:T(8,128)(2,1)} %broadcast_in_dim.2), calls=%async_computation.4 | async-start | bytes 8388608 | tf_op jit(solution)/shard_map/all_to_all | solution.py:67
  278.6 13.7 %all-to-all-start.3 = ((bf16[8,256,128]{2,1,0:T(8,128)(2,1)}), bf16[8,256,128]{2,1,0:T(8,128)(2,1)S(1)}, u32[]{:S(2)}, u32[]{:S(2)}) async-start(bf16[8,256,128]{2,1,0:T(8,128)(2,1)} %bitcast.40), calls=%async_computation.3 | async-start | bytes 1048576 | tf_op jit(solution)/shard_map/all_to_all | solution.py:67
  (43 other events, 340.7 us)
Sparse Core Ops, SparseCore 0:
  23.5 61.5 all-gather.2
  93.7 46.5 all-gather.4

commit v2 on v1

--- a/solution.py
+++ b/solution.py
@@ -1,4 +1,3 @@
-import functools
 import math
 
 import jax
@@ -92,10 +91,17 @@
     return lax.dot_general(a, b, (((1,), (1,)), ((), ())), preferred_element_type=F32)
 
 
-def norm_kernel(place, patches, _after, normed, half):
-    wide = patches[...].astype(F32)
-    mean = jnp.mean(wide * wide, axis=-1, keepdims=True)
-    normed[...] = (wide * lax.rsqrt(mean + EPS)).astype(BF)
+def norm_kernel(place, patches, normed, half):
+    chunk = 32
+
+    def body(i, carry):
+        at = pl.ds(pl.multiple_of(i * chunk, chunk), chunk)
+        wide = patches[at].astype(F32)
+        mean = jnp.mean(wide * wide, axis=-1, keepdims=True)
+        normed[at] = (wide * lax.rsqrt(mean + EPS)).astype(BF)
+        return carry
+
+    lax.fori_loop(0, patches.shape[0] // chunk, body, 0)
     half[...] = normed[pl.ds(pl.multiple_of(place[2] * half.shape[0], half.shape[0]), half.shape[0])]
 
 
@@ -149,11 +155,11 @@
     )(states, w_qs, w_qc, w_k, w_v)
 
 
-def window_kernel(base, place, query, kv, before, out, stacked):
-    step = pl.program_id(0) + base
+def window_kernel(place, query, kv, before, out, stacked):
+    step = pl.program_id(0)
     cols = query.shape[1]
 
-    @pl.when(step == base)
+    @pl.when(step == 0)
     def _():
         stacked[:WINDOW] = before[...]
         stacked[WINDOW:] = kv[...]
@@ -187,31 +193,29 @@
         out[:, lanes] = dot(w, values).astype(BF)
 
 
-def window_attention(place, query, kv, before, part):
+def window_attention(place, query, kv, before):
     count, cols = query.shape
-    steps = count // QROWS // 2
-    first = part * steps
     block = pl.BlockSpec((QROWS, cols), lambda i: (i, 0))
     return pl.pallas_call(
-        functools.partial(window_kernel, first),
-        out_shape=sds((count // 2, cols), BF),
-        grid=(steps,),
+        window_kernel,
+        out_shape=sds((count, cols), BF),
+        grid=(count // QROWS,),
         in_specs=[
             pl.BlockSpec(memory_space=pltpu.SMEM),
-            pl.BlockSpec((QROWS, cols), lambda i: (i + first, 0)),
+            block,
             pl.BlockSpec(kv.shape, lambda i: (0, 0)),
             pl.BlockSpec(before.shape, lambda i: (0, 0)),
         ],
         out_specs=block,
         scratch_shapes=[pltpu.VMEM((WINDOW + count, 2 * cols), BF)],
-        cost_estimate=cost(7),
+        cost_estimate=cost(14),
     )(place, query, kv, before)
 
 
 def ffn_kernel(place, *refs):
     pieces, gate_up = refs[:9], refs[9]
     outs = refs[10:14]
-    rows_buf, weight_buf, sems = refs[14:]
+    rows_buf, weight_buf, hidden, sems = refs[14:]
     core = place[2]
     rows = pieces[0].shape[0]
     half, quarter = rows // 2, rows // 4
@@ -221,22 +225,26 @@
         starts += [slab * rows + own, slab * rows + other]
     starts += [3 * rows + own, 3 * rows + own + quarter]
     starts += [3 * rows + other, 3 * rows + other + quarter]
-    weight_copy = pltpu.make_async_copy(gate_up, weight_buf, sems.at[9])
+    weight_copy = pltpu.make_async_copy(gate_up, weight_buf, sems.at[NY])
     weight_copy.start()
-    copies = []
-    for i, piece in enumerate(pieces):
-        size = piece.shape[0]
-        at = pl.multiple_of(starts[i], quarter)
-        copies.append(pltpu.make_async_copy(piece, rows_buf.at[pl.ds(at, size)], sems.at[i]))
-        copies[-1].start()
+    for start, slab, piece in zip(starts, (0, 1, 1, 2, 2, 3, 3, 3, 3), pieces):
+        at = pl.multiple_of(start, quarter)
+        target = rows_buf.at[pl.ds(at, piece.shape[0])]
+        pltpu.make_async_copy(piece, target, sems.at[slab]).start()
     slot = outs[0].shape[1]
     weight_copy.wait()
-    for slab, used in enumerate(((0,), (1, 2), (3, 4), (5, 6, 7, 8))):
-        for i in used:
-            copies[i].wait()
-        sums = dot(rows_buf[slab * rows : (slab + 1) * rows], weight_buf[...])
+
+    def body(slab, carry):
+        view = rows_buf.at[pl.ds(pl.multiple_of(slab * rows, rows), rows)]
+        pltpu.make_async_copy(view, view, sems.at[slab]).wait()
+        sums = dot(view[...], weight_buf[...])
         gate = sums[:, :slot]
-        outs[slab][...] = (gate * (1.0 / (1.0 + jnp.exp(-gate))) * sums[:, slot:]).astype(BF)
+        hidden[slab] = (gate * (1.0 / (1.0 + jnp.exp(-gate))) * sums[:, slot:]).astype(BF)
+        return carry
+
+    lax.fori_loop(0, NY, body, 0)
+    for slab in range(NY):
+        outs[slab][...] = hidden[slab]
 
 
 def edge_kernel(place, own, after, before, far, head, tail):
@@ -255,13 +263,18 @@
     hid[:, HALO + rows :] = below[...]
     keep = mix.shape[0] // NY
     cols = out.shape[2]
-    for f in range(NF):
+
+    def body(f, carry):
+        lanes = pl.ds(pl.multiple_of(f * cols, cols), cols)
         total = None
         for block in range(NY):
-            piece = mix[block * keep : (block + 1) * keep, f * cols : (f + 1) * cols]
+            piece = mix[block * keep : (block + 1) * keep, lanes]
             term = dot(hid[block, :, :keep], piece)
             total = term if total is None else total + term
         out[f] = total.astype(BF)
+        return carry
+
+    lax.fori_loop(0, NF, body, 0)
 
 
 def keys_kernel(parts, own, above, below, kv):
@@ -278,7 +291,8 @@
     shape = (total, query.shape[0])
     index = lax.broadcasted_iota(jnp.int32, shape, 0) + (place[3] * rows - HALO)
     held = byte_patch[...]
-    mask = (index <= held) & (index > held - PWIN) & (index >= 0)
+    mask = (index <= held) & (index > jnp.maximum(held - PWIN, -1))
+    contexts = []
     for head in range(cols // HD):
         q = query[:, head * HD : (head + 1) * HD] * SCALE
         s = dot_nt(stacked[:, head * HD : (head + 1) * HD], q)
@@ -289,7 +303,8 @@
         context = lax.dot_general(
             values, w, (((0,), (0,)), ((), ())), preferred_element_type=F32
         )
-        out[:, head * HD : (head + 1) * HD] = context.T.astype(BF)
+        contexts.append(context)
+    out[...] = jnp.concatenate(contexts, axis=0).T.astype(BF)
 
 
 def cross_attention(place, query, byte_patch, kv):
@@ -380,9 +395,7 @@
         norm_kernel,
         (sds((rows, width), BF), sds((rows // NC, width), BF)),
         patches,
-        gate_up,
         scalars=place,
-        anywhere=(1,),
     )
     gate_up = lax.all_gather(gate_up, "z", axis=0, tiled=True)
     down_t = swap(down_weight.T.reshape(NZ, hid_z, d_rows), "z")
@@ -422,11 +435,8 @@
 
     query_s, query_c, both_s = project(byte_states, self_query, cross_query, self_key, self_value)
     tail = lax.ppermute(both_s[byte_count - WINDOW :], SEQ, steps)
-    halves = []
-    for half in range(2):
-        halves.append(window_attention(place, query_s, both_s, tail, half))
-    context_s = jnp.concatenate(halves).reshape(NF, chunk, head_cols)
-    context_s = swap(context_s, FFN)
+    context_s = window_attention(place, query_s, both_s, tail)
+    context_s = swap(context_s.reshape(NF, chunk, head_cols), FFN)
     self_part = call(self_part_kernel, sds((chunk, NF * head_cols), F32), context_s, outs)
     piece = sds((rows, slot), BF)
     h_own, h_after, h_before, h_far = call(
@@ -439,7 +449,7 @@
         scratch=(
             pltpu.VMEM((NY * rows, width), BF),
             pltpu.VMEM(gate_up.shape, BF),
-            pltpu.SemaphoreType.DMA((10,)),
+            pltpu.VMEM((NY, rows, slot), BF), pltpu.SemaphoreType.DMA((NY + 1,)),
         ),
     )
     hid_after = lax.ppermute(h_before, "y", DOWN)
@@ -500,4 +510,6 @@
         P(FFN, None),
         P(FFN, None),
     )
-    return jax.shard_map(local, mesh=fine, in_specs=placed, out_specs=P(SEQ, FFN), check_vma=False)
+    return jax.shard_map(
+        local, mesh=fine, in_specs=placed, out_specs=P(SEQ, FFN), check_vma=False
+    )

time: 322 us -> 324 us (level)
  waiting for transfers between devices: 113 us -> 121 us
    ppermute x9, starting transfers between devices: 12.1 us -> 16.7 us  [other_core(): return lax.ppermute(value, 'c', [(0, 1), (1, 0)])]
    ppermute x3, waiting for transfers between devices: 1.22 us -> 5.2 us  [ring(): far_low = lax.ppermute(before[:half], axis, UP)]
    pallas_call x2 -> x1, Pallas kernels: 14.9 us -> 12.8 us  [window_attention(): pl.pallas_call(window_kernel, out_shape=sds((count, cols), BF), grid=(cou...]
    unnamed x66 -> x60, local copies, waits for them, and re-layouts: 12.2 us -> 11.5 us
  transfers between devices with their start and end apart: 36 -> 36, of which waited for: 12 -> 14; matrix products, arithmetic and copies ran while one was open for 3% -> 2% of each run, Pallas kernels for 19% -> 18%
where the time goes in v2:
time: 324 us; the launch traced here: 322 us
  waiting for transfers between devices  121 us (37%)
  starting transfers between devices  77.1 us (24%)
  Pallas kernels  63.8 us (20%)
  blocking collectives  27.1 us (8%)
  local copies, waits for them, and re-layouts  17.1 us (5%)
  between operations  13.8 us (4%)
    all_to_all x5, waiting for transfers between devices, swap(): return lax.all_to_all(value, axes, split_axis=0, concat_axis=0, tiled=True)  66 us
    pallas_call x9, Pallas kernels, call(): pl.pallas_call(kernel, out_shape=out, in_specs=specs, out_specs=jax.tree....  38.8 us
    ppermute x3, waiting for transfers between devices, ring(): before = lax.ppermute(value, axis, UP)  37.6 us
    all_to_all x5, starting transfers between devices, swap(): return lax.all_to_all(value, axes, split_axis=0, concat_axis=0, tiled=True)  28.9 us
    all_to_all x2, blocking collectives, swap(): return lax.all_to_all(value, axes, split_axis=0, concat_axis=0, tiled=True)  27.1 us
    ppermute x9, starting transfers between devices, other_core(): return lax.ppermute(value, 'c', [(0, 1), (1, 0)])  16.7 us
    pallas_call x1, Pallas kernels, window_attention(): pl.pallas_call(window_kernel, out_shape=sds((count, cols), BF), grid=(cou...  12.8 us
    unnamed x60, local copies, waits for them, and re-layouts  11.5 us
  transfers between devices with their start and end apart: 36, of which 14 were waited for; matrix products, arithmetic and copies ran while one was open for 2% of the time, Pallas kernels for 18%

profile of v2, /device:TPU:1, one launch (start us, length us, event | category | flops | bytes accessed | tf_op | source)
XLA Modules:
  0.0 322.4 jit_solution(2191466103724730878)
XLA Ops:
  8.9 13.4 %all_to_all.35 = bf16[4,128,512]{1,2,0:T(8,128)(2,1)S(1)} all-to-all(bf16[4,128,512]{1,2,0:T(8,128)(2,1)S(1)} %fusion.2), channel_id=1, replica_groups=mesh['z'=8,'y'=4,'x'=4,'c'=2] {'y'}, dimensions={0} | all-to-all | bytes 1048576 | tf_op jit(solution)/shard_map/all_to_all | solution.py:66
  29.7 7.8 %collective-permute-done.13.refs_1_ = bf16[1024,256]{1,0:T(8,128)(2,1)S(1)} collective-permute-done((bf16[1024,256]{1,0:T(8,128)(2,1)S(1)}, bf16[1024,256]{1,0:T(8,128)(2,1)S(1)}, u32[]{:S(2)}, u32[]{:S(2)}) %collective-permute-start.13) | collective-permute-done | bytes 524320 | tf_op jit(solution)/shard_map/ppermute | solution.py:75
  44.3 8.2 %all-to-all-start.1 = ((bf16[8,112,128]{2,1,0:T(8,128)(2,1)}), bf16[8,112,128]{2,1,0:T(8,128)(2,1)S(1)}, u32[]{:S(2)}, u32[]{:S(2)}) async-start(bf16[8,112,128]{2,1,0:T(8,128)(2,1)} %bitcast.11), calls=%async_computation.1 | async-start | bytes 458752 | tf_op jit(solution)/shard_map/all_to_all | solution.py:66
  54.3 11.9 %all-to-all-done.1.down_t = bf16[8,112,128]{2,1,0:T(8,128)(2,1)S(1)} async-done(((bf16[8,112,128]{2,1,0:T(8,128)(2,1)}), bf16[8,112,128]{2,1,0:T(8,128)(2,1)S(1)}, u32[]{:S(2)}, u32[]{:S(2)}) %all-to-all-start.1) | async-done | bytes 229408 | tf_op jit(solution)/shard_map/all_to_all | solution.py:66
  74.2 9.4 %collective-permute-done.22.before = bf16[112,2048]{1,0:T(8,128)(2,1)S(1)} collective-permute-done((bf16[112,2048]{1,0:T(8,128)(2,1)}, bf16[112,2048]{1,0:T(8,128)(2,1)S(1)}, u32[]{:S(2)}, u32[]{:S(2)}) %collective-permute-start.22) | collective-permute-done | bytes 458784 | tf_op jit(solution)/shard_map/ppermute | solution.py:75
  93.6 4.5 %shard_map.137 = (bf16[256,4096]{1,0:T(8,128)(2,1)}, bf16[128,4096]{1,0:T(8,128)(2,1)}) custom-call(s32[4]{0:T(128)} %pad_add_fusion.place, bf16[256,4096]{1,0:T(8,128)(2,1)} %patches.1), custom_call_target="tpu_custom_call" | custom-call | flops 2400000000 | bytes 10000000 | tf_op jit(solution)/shard_map/pallas_call | solution.py:55
  100.8 20.4 %collective-permute-done.2.refs_3_ = bf16[128,4096]{1,0:T(8,128)(2,1)S(1)} collective-permute-done((bf16[128,4096]{1,0:T(8,128)(2,1)}, bf16[128,4096]{1,0:T(8,128)(2,1)S(1)}, u32[]{:S(2)}, u32[]{:S(2)}) %collective-permute-start.2) | collective-permute-done | bytes 1048608 | tf_op jit(solution)/shard_map/ppermute | solution.py:75
  132.2 4.8 %collective-permute-start.6 = (bf16[64,4096]{1,0:T(8,128)(2,1)}, bf16[64,4096]{1,0:T(8,128)(2,1)}, u32[]{:S(2)}, u32[]{:S(2)}) collective-permute-start(bf16[64,4096]{1,0:T(8,128)(2,1)} %collective-permute-done.4.refs_5_), channel_id=1, source_target_pairs={{0,1},{1,0},{2,3},{3,2},{4,5},{5,4},{6,7},{7,6},{8,9},{9,8},{10,11... | collective-permute-start | bytes 1572872 | tf_op jit(solution)/shard_map/ppermute | solution.py:83
  140.6 6.0 %shard_map.136 = (bf16[2048,128]{1,0:T(8,128)(2,1)}, bf16[2048,128]{1,0:T(8,128)(2,1)}, bf16[2048,256]{1,0:T(8,128)(2,1)}) custom-call(bf16[2048,1024]{1,0:T(8,128)(2,1)} %states.1, bf16[1024,128]{1,0:T(8,128)(2,1)} %w_qs.1, bf16[1024,128]{1,0:T(8,128)(2,1)} %w_qc.1, bf16[1024,128]{1,0:T(8,128)(2,1)} %w_k.1, bf16[1024,128]{1,0:T(8,128)(2,1)} %w_v.1), custom_call_target="tpu_custom_call" | custom-call | flops 3600000000 | bytes 15000000 | tf_op jit(solution)/shard_map/pallas_call | solution.py:148
  147.5 4.1 %collective-permute-start.28 = (bf16[512,256]{1,0:T(8,128)(2,1)S(1)}, bf16[512,256]{1,0:T(8,128)(2,1)}, u32[]{:S(2)}, u32[]{:S(2)}) collective-permute-start(bf16[512,256]{1,0:T(8,128)(2,1)S(1)} %slice.35), channel_id=1, source_target_pairs={{0,8},{8,16},{16,24},{24,32},{32,40},{40,48},{48,56},{56,64},{64,7... | collective-permute-start | bytes 786440 | tf_op jit(solution)/shard_map/ppermute | solution.py:437
  151.7 9.5 %shard_map.138 = (bf16[256,256]{1,0:T(8,128)(2,1)}, bf16[256,256]{1,0:T(8,128)(2,1)}, bf16[256,256]{1,0:T(8,128)(2,1)}, bf16[256,256]{1,0:T(8,128)(2,1)}) custom-call(s32[4]{0:T(128)} %pad_add_fusion.place, bf16[256,4096]{1,0:T(8,128)(2,1)} %get-tuple-element.17.refs_0_, bf16[128,4096]{1,0:T(8,128)(2,1)} %copy-done.2, ...), custom_call_target="tpu_custom_call" | custom-call | flops 2400000000 | bytes 10000000 | tf_op jit(solution)/shard_map/pallas_call | solution.py:55
  165.3 12.8 %shard_map.145 = bf16[2048,128]{1,0:T(8,128)(2,1)} custom-call(s32[4]{0:T(128)} %pad_add_fusion.place, bf16[2048,128]{1,0:T(8,128)(2,1)} %get-tuple-element.25.query, bf16[2048,256]{1,0:T(8,128)(2,1)} %get-tuple-element.26.kv, bf16[512,256]{1,0:T(8,128)(2,1)} %collective-permute-done.28.before), custom_call_target="tpu_custom_call" | custom-call | flops 8400000000 | bytes 35000000 | tf_op jit(solution)/shard_map/pallas_call | solution.py:199
  178.1 4.5 %all-to-all-start.5 = ((bf16[8,256,128]{2,1,0:T(8,128)(2,1)}), bf16[8,256,128]{2,1,0:T(8,128)(2,1)S(1)}, u32[]{:S(2)}, u32[]{:S(2)}) async-start(bf16[8,256,128]{2,1,0:T(8,128)(2,1)} %bitcast.39), calls=%async_computation.5 | async-start | bytes 1048576 | tf_op jit(solution)/shard_map/all_to_all | solution.py:66
  193.2 6.3 %shard_map.142 = bf16[8,320,256]{2,1,0:T(8,128)(2,1)} custom-call(s32[4]{0:T(128)} %pad_add_fusion.place, bf16[256,256]{1,0:T(8,128)(2,1)} %get-tuple-element.19.own, bf16[256,256]{1,0:T(8,128)(2,1)} %copy-done.21, bf16[256,256]{1,0:T(8,128)(2,1)} %copy-done.22, bf16[256,256]{1,0:T(8,128)(2,1)} %copy-done.23, bf16[4,32,256]{2,1,0:T(8,128)(2,1)} %copy-done.24, ...), custom_call_target="tpu_custom_call" | custom-call | flops 2400000000 | bytes 10000000 | tf_op jit(solution)/shard_map/pallas_call | solution.py:55
  200.4 6.3 %all-to-all-start.2 = ((bf16[8,320,256]{2,1,0:T(8,128)(2,1)}), bf16[8,320,256]{2,1,0:T(8,128)(2,1)S(1)}, u32[]{:S(2)}, u32[]{:S(2)}) async-start(bf16[8,320,256]{2,1,0:T(8,128)(2,1)} %shard_map.142), calls=%async_computation.2 | async-start | bytes 2621440 | tf_op jit(solution)/shard_map/all_to_all | solution.py:66
  206.7 17.7 %all-to-all-done.2.parts = bf16[8,320,256]{2,1,0:T(8,128)(2,1)S(1)} async-done(((bf16[8,320,256]{2,1,0:T(8,128)(2,1)}), bf16[8,320,256]{2,1,0:T(8,128)(2,1)S(1)}, u32[]{:S(2)}, u32[]{:S(2)}) %all-to-all-start.2) | async-done | bytes 1310752 | tf_op jit(solution)/shard_map/all_to_all | solution.py:66
  228.1 5.6 %all-to-all-start.4 = ((bf16[8,256,1024]{2,1,0:T(8,128)(2,1)}), bf16[8,256,1024]{2,1,0:T(8,128)(2,1)}, u32[]{:S(2)}, u32[]{:S(2)}) async-start(bf16[8,256,1024]{2,1,0:T(8,128)(2,1)} %broadcast_in_dim.2), calls=%async_computation.4 | async-start | bytes 8388608 | tf_op jit(solution)/shard_map/all_to_all | solution.py:66
  245.2 6.1 %shard_map.144 = bf16[2048,128]{1,0:T(8,128)(2,1)} custom-call(s32[4]{0:T(128)} %pad_add_fusion.place, bf16[2048,128]{1,0:T(8,128)(2,1)} %get-tuple-element.16.query, s32[1,2048]{1,0:T(1,128)} %bitcast.42, bf16[320,256]{1,0:T(8,128)(2,1)} %shard_map.143.stacked), custom_call_target="tpu_custom_call" | custom-call | flops 3600000000 | bytes 15000000 | tf_op jit(solution)/shard_map/pallas_call | solution.py:313
  251.4 31.1 %all-to-all-done.4 = bf16[8,256,1024]{2,1,0:T(8,128)(2,1)} async-done(((bf16[8,256,1024]{2,1,0:T(8,128)(2,1)}), bf16[8,256,1024]{2,1,0:T(8,128)(2,1)}, u32[]{:S(2)}, u32[]{:S(2)}) %all-to-all-start.4) | async-done | bytes 4194336 | tf_op jit(solution)/shard_map/all_to_all | solution.py:66
  282.4 4.4 %all-to-all-start.3 = ((bf16[8,256,128]{2,1,0:T(8,128)(2,1)}), bf16[8,256,128]{2,1,0:T(8,128)(2,1)S(1)}, u32[]{:S(2)}, u32[]{:S(2)}) async-start(bf16[8,256,128]{2,1,0:T(8,128)(2,1)} %bitcast.40), calls=%async_computation.3 | async-start | bytes 1048576 | tf_op jit(solution)/shard_map/all_to_all | solution.py:66
  286.8 4.1 %shard_map.146.self_part = f32[256,1024]{1,0:T(8,128)} custom-call(bf16[8,256,128]{2,1,0:T(8,128)(2,1)} %copy-done.6, bf16[2048,1024]{1,0:T(8,128)(2,1)} %bitcast.16.outs), custom_call_target="tpu_custom_call" | custom-call | flops 2400000000 | bytes 10000000 | tf_op jit(solution)/shard_map/pallas_call | solution.py:55
  290.9 5.3 %all-to-all-done.3.context = bf16[8,256,128]{2,1,0:T(8,128)(2,1)S(1)} async-done(((bf16[8,256,128]{2,1,0:T(8,128)(2,1)}), bf16[8,256,128]{2,1,0:T(8,128)(2,1)S(1)}, u32[]{:S(2)}, u32[]{:S(2)}) %all-to-all-start.3) | async-done | bytes 524320 | tf_op jit(solution)/shard_map/all_to_all | solution.py:66
  297.0 4.2 %shard_map.147 = bf16[8,256,128]{2,1,0:T(8,128)(2,1)} custom-call(bf16[8,256,128]{2,1,0:T(8,128)(2,1)} %copy-done.8, bf16[2048,1024]{1,0:T(8,128)(2,1)} %bitcast.16.outs, f32[256,1024]{1,0:T(8,128)} %shard_map.146.self_part), custom_call_target="tpu_custom_call" | custom-call | flops 2400000000 | bytes 10000000 | tf_op jit(solution)/shard_map/pallas_call | solution.py:55
  301.1 13.7 %all_to_all.36 = bf16[8,256,128]{2,1,0:T(8,128)(2,1)S(1)} all-to-all(bf16[8,256,128]{2,1,0:T(8,128)(2,1)} %shard_map.147), channel_id=1, replica_groups=mesh['z'=8,'y'=4,'x'=4,'c'=2] {'x','c'}, dimensions={0} | all-to-all | bytes 1048576 | tf_op jit(solution)/shard_map/all_to_all | solution.py:66
  (142 shorter events, 86.7 us)
Async XLA Ops:
  6.5 145.1 %all-gather.3.cloned.1.call-start = ((), (), s32[]{:S(2)}) async-start(), calls=%async_computation.7 | async-start | bytes 4718592 | tf_op jit(solution)/shard_map/all_gather | solution.py:400
  24.5 13.0 %collective-permute-start.13 = (bf16[1024,256]{1,0:T(8,128)(2,1)S(1)}, bf16[1024,256]{1,0:T(8,128)(2,1)S(1)}, u32[]{:S(2)}, u32[]{:S(2)}) collective-permute-start(bf16[1024,256]{1,0:T(8,128)(2,1)S(1)} %bitcast.35), channel_id=1, source_target_pairs={{0,2},{2,4},{4,6},{6,0},{1,3},{3,5},{5,7},{7,1},{8,10},{10,12},{12... | collective-permute-start | bytes 1572872 | tf_op jit(solution)/shard_map/ppermute | solution.py:75
  25.8 14.7 %collective-permute-start.14 = (bf16[1024,256]{1,0:T(8,128)(2,1)S(1)}, bf16[1024,256]{1,0:T(8,128)(2,1)S(1)}, u32[]{:S(2)}, u32[]{:S(2)}) collective-permute-start(bf16[1024,256]{1,0:T(8,128)(2,1)S(1)} %bitcast.36), channel_id=1, source_target_pairs={{0,6},{2,0},{4,2},{6,4},{1,7},{3,1},{5,3},{7,5},{8,14},{10,8},{12,... | collective-permute-start | bytes 1572872 | tf_op jit(solution)/shard_map/ppermute | solution.py:76
  27.3 38.9 %collective-permute-start.17 = (bf16[1024,256]{1,0:T(8,128)(2,1)S(1)}, bf16[1024,256]{1,0:T(8,128)(2,1)}, u32[]{:S(2)}, u32[]{:S(2)}) collective-permute-start(bf16[1024,256]{1,0:T(8,128)(2,1)S(1)} %bitcast.37), channel_id=1, source_target_pairs={{0,1},{1,0},{2,3},{3,2},{4,5},{5,4},{6,7},{7,6},{8,9},{9,8},{10,11... | collective-permute-start | bytes 1572872 | tf_op jit(solution)/shard_map/ppermute | solution.py:83
  37.5 15.0 %collective-permute-start.15 = (bf16[512,256]{1,0:T(8,128)(2,1)S(1)}, bf16[512,256]{1,0:T(8,128)(2,1)}, u32[]{:S(2)}, u32[]{:S(2)}) collective-permute-start(bf16[512,256]{1,0:T(8,128)(2,1)S(1)} %slice.38), channel_id=1, source_target_pairs={{0,2},{2,4},{4,6},{6,0},{1,3},{3,5},{5,7},{7,1},{8,10},{10,12},{12... | collective-permute-start | bytes 786440 | tf_op jit(solution)/shard_map/ppermute | solution.py:77
  37.6 28.6 %collective-permute-start.18 = (bf16[1024,256]{1,0:T(8,128)(2,1)S(1)}, bf16[1024,256]{1,0:T(8,128)(2,1)}, u32[]{:S(2)}, u32[]{:S(2)}) collective-permute-start(bf16[1024,256]{1,0:T(8,128)(2,1)S(1)} %collective-permute-done.13.refs_1_), channel_id=1, source_target_pairs={{0,1},{1,0},{2,3},{3,2},{4,5},{5,4},{6,7},{7,6},{8,9},{9,8},{10,11... | collective-permute-start | bytes 1572872 | tf_op jit(solution)/shard_map/ppermute | solution.py:83
  40.6 25.6 %collective-permute-start.19 = (bf16[1024,256]{1,0:T(8,128)(2,1)S(1)}, bf16[1024,256]{1,0:T(8,128)(2,1)}, u32[]{:S(2)}, u32[]{:S(2)}) collective-permute-start(bf16[1024,256]{1,0:T(8,128)(2,1)S(1)} %collective-permute-done.14.refs_2_), channel_id=1, source_target_pairs={{0,1},{1,0},{2,3},{3,2},{4,5},{5,4},{6,7},{7,6},{8,9},{9,8},{10,11... | collective-permute-start | bytes 1572872 | tf_op jit(solution)/shard_map/ppermute | solution.py:83
  44.3 21.9 %all-to-all-start.1 = ((bf16[8,112,128]{2,1,0:T(8,128)(2,1)}), bf16[8,112,128]{2,1,0:T(8,128)(2,1)S(1)}, u32[]{:S(2)}, u32[]{:S(2)}) async-start(bf16[8,112,128]{2,1,0:T(8,128)(2,1)} %bitcast.11), calls=%async_computation.1 | async-start | bytes 458752 | tf_op jit(solution)/shard_map/all_to_all | solution.py:66
  52.5 140.1 %all-gather.5.cloned.1.call-start = ((), (), s32[]{:S(2)}) async-start(), calls=%async_computation.8 | async-start | bytes 4128768 | tf_op jit(solution)/shard_map/all_gather | solution.py:425
  52.5 13.7 %collective-permute-start.20 = (bf16[512,256]{1,0:T(8,128)(2,1)}, bf16[512,256]{1,0:T(8,128)(2,1)S(1)}, u32[]{:S(2)}, u32[]{:S(2)}) collective-permute-start(bf16[512,256]{1,0:T(8,128)(2,1)} %collective-permute-done.15.refs_3_), channel_id=1, source_target_pairs={{0,1},{1,0},{2,3},{3,2},{4,5},{5,4},{6,7},{7,6},{8,9},{9,8},{10,11... | collective-permute-start | bytes 786440 | tf_op jit(solution)/shard_map/ppermute | solution.py:83
  98.2 23.1 %collective-permute-start.2 = (bf16[128,4096]{1,0:T(8,128)(2,1)}, bf16[128,4096]{1,0:T(8,128)(2,1)S(1)}, u32[]{:S(2)}, u32[]{:S(2)}) collective-permute-start(bf16[128,4096]{1,0:T(8,128)(2,1)} %get-tuple-element.18), channel_id=1, source_target_pairs={{0,8},{8,16},{16,24},{24,0},{1,9},{9,17},{17,25},{25,1},{2,10},{10... | collective-permute-start | bytes 3145736 | tf_op jit(solution)/shard_map/ppermute | solution.py:75
  98.2 27.2 %collective-permute-start = (bf16[128,4096]{1,0:T(8,128)(2,1)}, bf16[128,4096]{1,0:T(8,128)(2,1)S(1)}, u32[]{:S(2)}, u32[]{:S(2)}) collective-permute-start(bf16[128,4096]{1,0:T(8,128)(2,1)} %get-tuple-element.18), channel_id=1, source_target_pairs={{0,24},{8,0},{16,8},{24,16},{1,25},{9,1},{17,9},{25,17},{2,26},{10... | collective-permute-start | bytes 3145736 | tf_op jit(solution)/shard_map/ppermute | solution.py:76
  121.4 30.2 %collective-permute-start.3 = (bf16[128,4096]{1,0:T(8,128)(2,1)S(1)}, bf16[128,4096]{1,0:T(8,128)(2,1)}, u32[]{:S(2)}, u32[]{:S(2)}) collective-permute-start(bf16[128,4096]{1,0:T(8,128)(2,1)S(1)} %collective-permute-done.2.refs_3_), channel_id=1, source_target_pairs={{0,1},{1,0},{2,3},{3,2},{4,5},{5,4},{6,7},{7,6},{8,9},{9,8},{10,11... | collective-permute-start | bytes 3145736 | tf_op jit(solution)/shard_map/ppermute | solution.py:83
  125.4 26.2 %collective-permute-start.1 = (bf16[128,4096]{1,0:T(8,128)(2,1)S(1)}, bf16[128,4096]{1,0:T(8,128)(2,1)}, u32[]{:S(2)}, u32[]{:S(2)}) collective-permute-start(bf16[128,4096]{1,0:T(8,128)(2,1)S(1)} %collective-permute-done.refs_1_), channel_id=1, source_target_pairs={{0,1},{1,0},{2,3},{3,2},{4,5},{5,4},{6,7},{7,6},{8,9},{9,8},{10,11... | collective-permute-start | bytes 3145736 | tf_op jit(solution)/shard_map/ppermute | solution.py:83
  125.5 13.8 %collective-permute-start.5 = (bf16[64,4096]{1,0:T(8,128)(2,1)S(1)}, bf16[64,4096]{1,0:T(8,128)(2,1)}, u32[]{:S(2)}, u32[]{:S(2)}) collective-permute-start(bf16[64,4096]{1,0:T(8,128)(2,1)S(1)} %slice.37), channel_id=1, source_target_pairs={{0,24},{8,0},{16,8},{24,16},{1,25},{9,1},{17,9},{25,17},{2,26},{10... | collective-permute-start | bytes 1572872 | tf_op jit(solution)/shard_map/ppermute | solution.py:78
  132.2 19.4 %collective-permute-start.6 = (bf16[64,4096]{1,0:T(8,128)(2,1)}, bf16[64,4096]{1,0:T(8,128)(2,1)}, u32[]{:S(2)}, u32[]{:S(2)}) collective-permute-start(bf16[64,4096]{1,0:T(8,128)(2,1)} %collective-permute-done.4.refs_5_), channel_id=1, source_target_pairs={{0,1},{1,0},{2,3},{3,2},{4,5},{5,4},{6,7},{7,6},{8,9},{9,8},{10,11... | collective-permute-start | bytes 1572872 | tf_op jit(solution)/shard_map/ppermute | solution.py:83
  147.5 17.7 %collective-permute-start.28 = (bf16[512,256]{1,0:T(8,128)(2,1)S(1)}, bf16[512,256]{1,0:T(8,128)(2,1)}, u32[]{:S(2)}, u32[]{:S(2)}) collective-permute-start(bf16[512,256]{1,0:T(8,128)(2,1)S(1)} %slice.35), channel_id=1, source_target_pairs={{0,8},{8,16},{16,24},{24,32},{32,40},{40,48},{48,56},{56,64},{64,7... | collective-permute-start | bytes 786440 | tf_op jit(solution)/shard_map/ppermute | solution.py:437
  161.1 21.4 %collective-permute-start.8 = (bf16[256,256]{1,0:T(8,128)(2,1)}, bf16[256,256]{1,0:T(8,128)(2,1)S(1)}, u32[]{:S(2)}, u32[]{:S(2)}) collective-permute-start(bf16[256,256]{1,0:T(8,128)(2,1)} %get-tuple-element.20), channel_id=1, source_target_pairs={{0,24},{8,0},{16,8},{24,16},{1,25},{9,1},{17,9},{25,17},{2,26},{10... | collective-permute-start | bytes 393224 | tf_op jit(solution)/shard_map/ppermute | solution.py:455
  162.6 20.0 %collective-permute-start.9 = (bf16[256,256]{1,0:T(8,128)(2,1)}, bf16[256,256]{1,0:T(8,128)(2,1)S(1)}, u32[]{:S(2)}, u32[]{:S(2)}) collective-permute-start(bf16[256,256]{1,0:T(8,128)(2,1)} %get-tuple-element.21), channel_id=1, source_target_pairs={{0,8},{8,16},{16,24},{24,0},{1,9},{9,17},{17,25},{25,1},{2,10},{10... | collective-permute-start | bytes 393224 | tf_op jit(solution)/shard_map/ppermute | solution.py:456
  162.7 19.9 %collective-permute-start.10 = (bf16[256,256]{1,0:T(8,128)(2,1)}, bf16[256,256]{1,0:T(8,128)(2,1)S(1)}, u32[]{:S(2)}, u32[]{:S(2)}) collective-permute-start(bf16[256,256]{1,0:T(8,128)(2,1)} %get-tuple-element.22), channel_id=1, source_target_pairs={{0,16},{8,24},{16,0},{24,8},{1,17},{9,25},{17,1},{25,9},{2,18},{10... | collective-permute-start | bytes 393224 | tf_op jit(solution)/shard_map/ppermute | solution.py:457
  178.1 21.5 %all-to-all-start.5 = ((bf16[8,256,128]{2,1,0:T(8,128)(2,1)}), bf16[8,256,128]{2,1,0:T(8,128)(2,1)S(1)}, u32[]{:S(2)}, u32[]{:S(2)}) async-start(bf16[8,256,128]{2,1,0:T(8,128)(2,1)} %bitcast.39), calls=%async_computation.5 | async-start | bytes 1048576 | tf_op jit(solution)/shard_map/all_to_all | solution.py:66
  200.4 24.0 %all-to-all-start.2 = ((bf16[8,320,256]{2,1,0:T(8,128)(2,1)}), bf16[8,320,256]{2,1,0:T(8,128)(2,1)S(1)}, u32[]{:S(2)}, u32[]{:S(2)}) async-start(bf16[8,320,256]{2,1,0:T(8,128)(2,1)} %shard_map.142), calls=%async_computation.2 | async-start | bytes 2621440 | tf_op jit(solution)/shard_map/all_to_all | solution.py:66
  228.1 54.4 %all-to-all-start.4 = ((bf16[8,256,1024]{2,1,0:T(8,128)(2,1)}), bf16[8,256,1024]{2,1,0:T(8,128)(2,1)}, u32[]{:S(2)}, u32[]{:S(2)}) async-start(bf16[8,256,1024]{2,1,0:T(8,128)(2,1)} %broadcast_in_dim.2), calls=%async_computation.4 | async-start | bytes 8388608 | tf_op jit(solution)/shard_map/all_to_all | solution.py:66
  282.4 13.7 %all-to-all-start.3 = ((bf16[8,256,128]{2,1,0:T(8,128)(2,1)}), bf16[8,256,128]{2,1,0:T(8,128)(2,1)S(1)}, u32[]{:S(2)}, u32[]{:S(2)}) async-start(bf16[8,256,128]{2,1,0:T(8,128)(2,1)} %bitcast.40), calls=%async_computation.3 | async-start | bytes 1048576 | tf_op jit(solution)/shard_map/all_to_all | solution.py:66
  (40 other events, 333.1 us)
Sparse Core Ops, SparseCore 0:
  23.5 61.5 all-gather.2
  93.8 46.3 all-gather.4

commit v3 on v2

--- a/solution.py
+++ b/solution.py
@@ -284,7 +284,7 @@
     kv[...] = total.astype(BF)
 
 
-def cross_kernel(place, query, byte_patch, stacked, out):
+def cross_kernel(place, query, byte_patch, stacked, context_s, out):
     total, both = stacked.shape
     cols = both // 2
     rows = total - 2 * HALO
@@ -304,42 +304,32 @@
             values, w, (((0,), (0,)), ((), ())), preferred_element_type=F32
         )
         contexts.append(context)
-    out[...] = jnp.concatenate(contexts, axis=0).T.astype(BF)
-
-
-def cross_attention(place, query, byte_patch, kv):
+    out[:, :cols] = jnp.concatenate(contexts, axis=0).T.astype(BF)
+    out[:, cols:] = context_s[...]
+
+
+def cross_attention(place, query, byte_patch, kv, context_s):
     count, cols = query.shape
     block = pl.BlockSpec((BROWS, cols), lambda i: (i, 0))
     return pl.pallas_call(
         cross_kernel,
-        out_shape=sds((count, cols), BF),
+        out_shape=sds((count, 2 * cols), BF),
         grid=(count // BROWS,),
         in_specs=[
             pl.BlockSpec(memory_space=pltpu.SMEM),
             block,
             pl.BlockSpec((1, BROWS), lambda i: (0, i)),
             pl.BlockSpec(kv.shape, lambda i: (0, 0)),
+            block,
         ],
-        out_specs=block,
+        out_specs=pl.BlockSpec((BROWS, 2 * cols), lambda i: (i, 0)),
         cost_estimate=cost(6),
-    )(place, query, byte_patch.reshape(1, count), kv)
-
-
-def out_product(context, outs, which):
-    both = outs.shape[0] // NF
-    half = both // 2
-    weight = jnp.concatenate(
-        [outs[f * both + which * half : f * both + (which + 1) * half] for f in range(NF)], axis=0
-    )
-    return dot(jnp.concatenate([context[f] for f in range(NF)], axis=1), weight)
-
-
-def self_part_kernel(context, outs, out):
-    out[...] = out_product(context, outs, 1)
-
-
-def update_kernel(context, outs, self_part, out):
-    total = (self_part[...] + out_product(context, outs, 0)).astype(BF)
+    )(place, query, byte_patch.reshape(1, count), kv, context_s)
+
+
+def update_kernel(context, outs, out):
+    total = dot(jnp.concatenate([context[f] for f in range(NF)], axis=1), outs[...])
+    total = total.astype(BF)
     cols = out.shape[2]
     for f in range(NF):
         out[f] = total[:, f * cols : (f + 1) * cols]
@@ -436,8 +426,7 @@
     query_s, query_c, both_s = project(byte_states, self_query, cross_query, self_key, self_value)
     tail = lax.ppermute(both_s[byte_count - WINDOW :], SEQ, steps)
     context_s = window_attention(place, query_s, both_s, tail)
-    context_s = swap(context_s.reshape(NF, chunk, head_cols), FFN)
-    self_part = call(self_part_kernel, sds((chunk, NF * head_cols), F32), context_s, outs)
+
     piece = sds((rows, slot), BF)
     h_own, h_after, h_before, h_far = call(
         ffn_kernel,
@@ -484,11 +473,9 @@
         own_below,
     )
 
-    context_c = cross_attention(place, query_c, byte_patch, both_c)
-    context_c = swap(context_c.reshape(NF, chunk, head_cols), FFN)
-    update = call(
-        update_kernel, sds((NF, chunk, head_cols), BF), context_c, outs, self_part
-    )
+    context = cross_attention(place, query_c, byte_patch, both_c, context_s)
+    context = swap(context.reshape(NF, chunk, both_cols), FFN)
+    update = call(update_kernel, sds((NF, chunk, head_cols), BF), context, outs)
     return swap(update, FFN).reshape(byte_count, head_cols)
 
 

time: 324 us -> 310 us (0.957)
  waiting for transfers between devices: 121 us -> 98 us
  blocking collectives: 27.1 us -> 47.3 us
  starting transfers between devices: 77.1 us -> 67.4 us
  Pallas kernels: 63.8 us -> 60.5 us
    all_to_all x5 -> x3, waiting for transfers between devices: 66 us -> 38.5 us  [swap(): return lax.all_to_all(value, axes, split_axis=0, concat_axis=0, tiled=True)]
    all_to_all x2 -> x3, blocking collectives: 27.1 us -> 47.3 us  [swap(): return lax.all_to_all(value, axes, split_axis=0, concat_axis=0, tiled=True)]
    all_to_all x5 -> x3, starting transfers between devices: 28.9 us -> 19.5 us  [swap(): return lax.all_to_all(value, axes, split_axis=0, concat_axis=0, tiled=True)]
    ppermute x1, waiting for transfers between devices: 0.01 us -> 6.01 us  [local(): hid_before = lax.ppermute(h_after, 'y', UP)]
    pallas_call x9 -> x8, Pallas kernels: 38.8 us -> 35.2 us  [call(): pl.pallas_call(kernel, out_shape=out, in_specs=specs, out_specs=jax.tree....]
    unnamed x60 -> x68, local copies, waits for them, and re-layouts: 11.5 us -> 11.7 us
  transfers between devices with their start and end apart: 36 -> 34, of which waited for: 14 -> 14; matrix products, arithmetic and copies ran while one was open for 2% -> 2% of each run, Pallas kernels for 18% -> 16%
where the time goes in v3:
time: 310 us; the launch traced here: 307 us
  waiting for transfers between devices  98 us (32%)
  starting transfers between devices  67.4 us (22%)
  Pallas kernels  60.5 us (20%)
  blocking collectives  47.3 us (15%)
  local copies, waits for them, and re-layouts  17.3 us (6%)
  between operations  13.8 us (4%)
    all_to_all x3, blocking collectives, swap(): return lax.all_to_all(value, axes, split_axis=0, concat_axis=0, tiled=True)  47.3 us
    all_to_all x3, waiting for transfers between devices, swap(): return lax.all_to_all(value, axes, split_axis=0, concat_axis=0, tiled=True)  38.5 us
    ppermute x3, waiting for transfers between devices, ring(): before = lax.ppermute(value, axis, UP)  37.6 us
    pallas_call x8, Pallas kernels, call(): pl.pallas_call(kernel, out_shape=out, in_specs=specs, out_specs=jax.tree....  35.2 us
    all_to_all x3, starting transfers between devices, swap(): return lax.all_to_all(value, axes, split_axis=0, concat_axis=0, tiled=True)  19.5 us
    ppermute x9, starting transfers between devices, other_core(): return lax.ppermute(value, 'c', [(0, 1), (1, 0)])  16.6 us
    pallas_call x1, Pallas kernels, window_attention(): pl.pallas_call(window_kernel, out_shape=sds((count, cols), BF), grid=(cou...  12.8 us
    unnamed x68, local copies, waits for them, and re-layouts  11.7 us
  transfers between devices with their start and end apart: 34, of which 14 were waited for; matrix products, arithmetic and copies ran while one was open for 2% of the time, Pallas kernels for 16%

profile of v3, /device:TPU:1, one launch (start us, length us, event | category | flops | bytes accessed | tf_op | source)
XLA Modules:
  0.0 307.3 jit_solution(14365831702317711538)
XLA Ops:
  8.9 13.4 %all_to_all.30 = bf16[4,128,512]{1,2,0:T(8,128)(2,1)S(1)} all-to-all(bf16[4,128,512]{1,2,0:T(8,128)(2,1)S(1)} %fusion.2), channel_id=1, replica_groups=mesh['z'=8,'y'=4,'x'=4,'c'=2] {'y'}, dimensions={0} | all-to-all | bytes 1048576 | tf_op jit(solution)/shard_map/all_to_all | solution.py:66
  29.7 7.8 %collective-permute-done.13.refs_1_ = bf16[1024,256]{1,0:T(8,128)(2,1)S(1)} collective-permute-done((bf16[1024,256]{1,0:T(8,128)(2,1)S(1)}, bf16[1024,256]{1,0:T(8,128)(2,1)S(1)}, u32[]{:S(2)}, u32[]{:S(2)}) %collective-permute-start.13) | collective-permute-done | bytes 524320 | tf_op jit(solution)/shard_map/ppermute | solution.py:75
  44.3 8.2 %all-to-all-start.1 = ((bf16[8,112,128]{2,1,0:T(8,128)(2,1)}), bf16[8,112,128]{2,1,0:T(8,128)(2,1)S(1)}, u32[]{:S(2)}, u32[]{:S(2)}) async-start(bf16[8,112,128]{2,1,0:T(8,128)(2,1)} %bitcast.11), calls=%async_computation.1 | async-start | bytes 458752 | tf_op jit(solution)/shard_map/all_to_all | solution.py:66
  54.4 11.8 %all-to-all-done.1.down_t = bf16[8,112,128]{2,1,0:T(8,128)(2,1)S(1)} async-done(((bf16[8,112,128]{2,1,0:T(8,128)(2,1)}), bf16[8,112,128]{2,1,0:T(8,128)(2,1)S(1)}, u32[]{:S(2)}, u32[]{:S(2)}) %all-to-all-start.1) | async-done | bytes 229408 | tf_op jit(solution)/shard_map/all_to_all | solution.py:66
  67.7 3.8 %shard_map.140.own = bf16[112,2048]{1,0:T(8,128)(2,1)} custom-call(s32[4]{0:T(128)} %pad_add_fusion.place, bf16[8,112,128]{2,1,0:T(8,128)(2,1)} %copy-done.15, bf16[1024,256]{1,0:T(8,128)(2,1)} %bitcast.38, bf16[1024,256]{1,0:T(8,128)(2,1)} %copy-done.17, bf16[1024,256]{1,0:T(8,128)(2,1)} %copy-done.18, bf16[512,256]{1,0:T(8,128)(2,1)} %collective-permute-done.15.refs_3_, ...), custom_call_target="tpu_custom_call" | custom-call | flops 2400000000 | bytes 10000000 | tf_op jit(solution)/shard_map/pallas_call | solution.py:55
  74.2 9.4 %collective-permute-done.22.before = bf16[112,2048]{1,0:T(8,128)(2,1)S(1)} collective-permute-done((bf16[112,2048]{1,0:T(8,128)(2,1)}, bf16[112,2048]{1,0:T(8,128)(2,1)S(1)}, u32[]{:S(2)}, u32[]{:S(2)}) %collective-permute-start.22) | collective-permute-done | bytes 458784 | tf_op jit(solution)/shard_map/ppermute | solution.py:75
  93.6 4.6 %shard_map.137 = (bf16[256,4096]{1,0:T(8,128)(2,1)}, bf16[128,4096]{1,0:T(8,128)(2,1)}) custom-call(s32[4]{0:T(128)} %pad_add_fusion.place, bf16[256,4096]{1,0:T(8,128)(2,1)} %patches.1), custom_call_target="tpu_custom_call" | custom-call | flops 2400000000 | bytes 10000000 | tf_op jit(solution)/shard_map/pallas_call | solution.py:55
  100.9 20.4 %collective-permute-done.2.refs_3_ = bf16[128,4096]{1,0:T(8,128)(2,1)S(1)} collective-permute-done((bf16[128,4096]{1,0:T(8,128)(2,1)}, bf16[128,4096]{1,0:T(8,128)(2,1)S(1)}, u32[]{:S(2)}, u32[]{:S(2)}) %collective-permute-start.2) | collective-permute-done | bytes 1048608 | tf_op jit(solution)/shard_map/ppermute | solution.py:75
  121.4 4.0 %collective-permute-start.3 = (bf16[128,4096]{1,0:T(8,128)(2,1)S(1)}, bf16[128,4096]{1,0:T(8,128)(2,1)S(1)}, u32[]{:S(2)}, u32[]{:S(2)}) collective-permute-start(bf16[128,4096]{1,0:T(8,128)(2,1)S(1)} %collective-permute-done.2.refs_3_), channel_id=1, source_target_pairs={{0,1},{1,0},{2,3},{3,2},{4,5},{5,4},{6,7},{7,6},{8,9},{9,8},{10,11... | collective-permute-start | bytes 3145736 | tf_op jit(solution)/shard_map/ppermute | solution.py:83
  128.5 3.8 %collective-permute-done.4.refs_5_ = bf16[64,4096]{1,0:T(8,128)(2,1)S(1)} collective-permute-done((bf16[64,4096]{1,0:T(8,128)(2,1)S(1)}, bf16[64,4096]{1,0:T(8,128)(2,1)S(1)}, u32[]{:S(2)}, u32[]{:S(2)}) %collective-permute-start.4) | collective-permute-done | bytes 524320 | tf_op jit(solution)/shard_map/ppermute | solution.py:77
  132.3 4.7 %collective-permute-start.6 = (bf16[64,4096]{1,0:T(8,128)(2,1)S(1)}, bf16[64,4096]{1,0:T(8,128)(2,1)S(1)}, u32[]{:S(2)}, u32[]{:S(2)}) collective-permute-start(bf16[64,4096]{1,0:T(8,128)(2,1)S(1)} %collective-permute-done.4.refs_5_), channel_id=1, source_target_pairs={{0,1},{1,0},{2,3},{3,2},{4,5},{5,4},{6,7},{7,6},{8,9},{9,8},{10,11... | collective-permute-start | bytes 1572872 | tf_op jit(solution)/shard_map/ppermute | solution.py:83
  142.8 9.5 %shard_map.138 = (bf16[256,256]{1,0:T(8,128)(2,1)}, bf16[256,256]{1,0:T(8,128)(2,1)}, bf16[256,256]{1,0:T(8,128)(2,1)}, bf16[256,256]{1,0:T(8,128)(2,1)}) custom-call(s32[4]{0:T(128)} %pad_add_fusion.place, bf16[256,4096]{1,0:T(8,128)(2,1)} %get-tuple-element.17.refs_0_, bf16[128,4096]{1,0:T(8,128)(2,1)} %copy-done.2, bf16[128,4096]{1,0:T(8,128)(2,1)} %copy-done.7, ...), custom_call_target="tpu_custom_call" | custom-call | flops 2400000000 | bytes 10000000 | tf_op jit(solution)/shard_map/pallas_call | solution.py:55
  158.7 6.0 %collective-permute-done.9.before = bf16[256,256]{1,0:T(8,128)(2,1)S(1)} collective-permute-done((bf16[256,256]{1,0:T(8,128)(2,1)}, bf16[256,256]{1,0:T(8,128)(2,1)S(1)}, u32[]{:S(2)}, u32[]{:S(2)}) %collective-permute-start.9) | collective-permute-done | bytes 131104 | tf_op jit(solution)/shard_map/ppermute | solution.py:445
  174.4 6.3 %shard_map.142 = bf16[8,320,256]{2,1,0:T(8,128)(2,1)} custom-call(s32[4]{0:T(128)} %pad_add_fusion.place, bf16[256,256]{1,0:T(8,128)(2,1)} %get-tuple-element.19.own, bf16[256,256]{1,0:T(8,128)(2,1)} %copy-done.25, bf16[256,256]{1,0:T(8,128)(2,1)} %copy-done.26, bf16[256,256]{1,0:T(8,128)(2,1)} %copy-done.27, bf16[4,32,256]{2,1,0:T(8,128)(2,1)} %copy-done.28, ...), custom_call_target="tpu_custom_call" | custom-call | flops 2400000000 | bytes 10000000 | tf_op jit(solution)/shard_map/pallas_call | solution.py:55
  180.7 5.9 %all-to-all-start.2 = ((bf16[8,320,256]{2,1,0:T(8,128)(2,1)}), bf16[8,320,256]{2,1,0:T(8,128)(2,1)S(1)}, u32[]{:S(2)}, u32[]{:S(2)}) async-start(bf16[8,320,256]{2,1,0:T(8,128)(2,1)} %shard_map.142), calls=%async_computation.2 | async-start | bytes 2621440 | tf_op jit(solution)/shard_map/all_to_all | solution.py:66
  186.6 17.8 %all-to-all-done.2.parts = bf16[8,320,256]{2,1,0:T(8,128)(2,1)S(1)} async-done(((bf16[8,320,256]{2,1,0:T(8,128)(2,1)}), bf16[8,320,256]{2,1,0:T(8,128)(2,1)S(1)}, u32[]{:S(2)}, u32[]{:S(2)}) %all-to-all-start.2) | async-done | bytes 1310752 | tf_op jit(solution)/shard_map/all_to_all | solution.py:66
  206.9 5.4 %all-to-all-start.4 = ((bf16[8,256,1024]{2,1,0:T(8,128)(2,1)}), bf16[8,256,1024]{2,1,0:T(8,128)(2,1)}, u32[]{:S(2)}, u32[]{:S(2)}) async-start(bf16[8,256,1024]{2,1,0:T(8,128)(2,1)} %broadcast_in_dim.2), calls=%async_computation.4 | async-start | bytes 8388608 | tf_op jit(solution)/shard_map/all_to_all | solution.py:66
  212.4 6.1 %shard_map.136 = (bf16[2048,128]{1,0:T(8,128)(2,1)}, bf16[2048,128]{1,0:T(8,128)(2,1)}, bf16[2048,256]{1,0:T(8,128)(2,1)}) custom-call(bf16[2048,1024]{1,0:T(8,128)(2,1)} %states.1, bf16[1024,128]{1,0:T(8,128)(2,1)} %w_qs.1, bf16[1024,128]{1,0:T(8,128)(2,1)} %w_qc.1, bf16[1024,128]{1,0:T(8,128)(2,1)} %w_k.1, bf16[1024,128]{1,0:T(8,128)(2,1)} %w_v.1), custom_call_target="tpu_custom_call" | custom-call | flops 3600000000 | bytes 15000000 | tf_op jit(solution)/shard_map/pallas_call | solution.py:148
  229.7 12.8 %shard_map.144.context_s = bf16[2048,128]{1,0:T(8,128)(2,1)} custom-call(s32[4]{0:T(128)} %pad_add_fusion.place, bf16[2048,128]{1,0:T(8,128)(2,1)} %get-tuple-element.25.query, bf16[2048,256]{1,0:T(8,128)(2,1)} %get-tuple-element.26.kv, bf16[512,256]{1,0:T(8,128)(2,1)} %copy-done.22), custom_call_target="tpu_custom_call" | custom-call | flops 8400000000 | bytes 35000000 | tf_op jit(solution)/shard_map/pallas_call | solution.py:199
  246.0 6.3 %shard_map.145 = bf16[2048,256]{1,0:T(8,128)(2,1)} custom-call(s32[4]{0:T(128)} %pad_add_fusion.place, bf16[2048,128]{1,0:T(8,128)(2,1)} %get-tuple-element.16.query, s32[1,2048]{1,0:T(1,128)} %bitcast.40, bf16[320,256]{1,0:T(8,128)(2,1)} %shard_map.143.stacked, bf16[2048,128]{1,0:T(8,128)(2,1)} %shard_map.144.context_s), custom_call_target="tpu_custom_call" | custom-call | flops 3600000000 | bytes 15000000 | tf_op jit(solution)/shard_map/pallas_call | solution.py:314
  252.3 8.9 %all-to-all-done.4 = bf16[8,256,1024]{2,1,0:T(8,128)(2,1)} async-done(((bf16[8,256,1024]{2,1,0:T(8,128)(2,1)}), bf16[8,256,1024]{2,1,0:T(8,128)(2,1)}, u32[]{:S(2)}, u32[]{:S(2)}) %all-to-all-start.4) | async-done | bytes 4194336 | tf_op jit(solution)/shard_map/all_to_all | solution.py:66
  261.2 20.1 %all_to_all.31.context = bf16[8,256,256]{2,1,0:T(8,128)(2,1)} all-to-all(bf16[8,256,256]{2,1,0:T(8,128)(2,1)} %bitcast.32), channel_id=1, replica_groups=mesh['z'=8,'y'=4,'x'=4,'c'=2] {'x','c'}, dimensions={0} | all-to-all | bytes 2097152 | tf_op jit(solution)/shard_map/all_to_all | solution.py:66
  281.3 4.6 %shard_map.146 = bf16[8,256,128]{2,1,0:T(8,128)(2,1)} custom-call(bf16[8,256,256]{2,1,0:T(8,128)(2,1)} %all_to_all.31.context, bf16[2048,1024]{1,0:T(8,128)(2,1)} %bitcast.16.outs), custom_call_target="tpu_custom_call" | custom-call | flops 2400000000 | bytes 10000000 | tf_op jit(solution)/shard_map/pallas_call | solution.py:55
  285.9 13.8 %all_to_all.32 = bf16[8,256,128]{2,1,0:T(8,128)(2,1)S(1)} all-to-all(bf16[8,256,128]{2,1,0:T(8,128)(2,1)} %shard_map.146), channel_id=1, replica_groups=mesh['z'=8,'y'=4,'x'=4,'c'=2] {'x','c'}, dimensions={0} | all-to-all | bytes 1048576 | tf_op jit(solution)/shard_map/all_to_all | solution.py:66
  (146 shorter events, 78.0 us)
Async XLA Ops:
  6.5 136.2 %all-gather.3.cloned.1.call-start = ((), (), s32[]{:S(2)}) async-start(), calls=%async_computation.6 | async-start | bytes 4718592 | tf_op jit(solution)/shard_map/all_gather | solution.py:390
  24.5 13.0 %collective-permute-start.13 = (bf16[1024,256]{1,0:T(8,128)(2,1)S(1)}, bf16[1024,256]{1,0:T(8,128)(2,1)S(1)}, u32[]{:S(2)}, u32[]{:S(2)}) collective-permute-start(bf16[1024,256]{1,0:T(8,128)(2,1)S(1)} %bitcast.35), channel_id=1, source_target_pairs={{0,2},{2,4},{4,6},{6,0},{1,3},{3,5},{5,7},{7,1},{8,10},{10,12},{12... | collective-permute-start | bytes 1572872 | tf_op jit(solution)/shard_map/ppermute | solution.py:75
  25.8 14.7 %collective-permute-start.14 = (bf16[1024,256]{1,0:T(8,128)(2,1)S(1)}, bf16[1024,256]{1,0:T(8,128)(2,1)S(1)}, u32[]{:S(2)}, u32[]{:S(2)}) collective-permute-start(bf16[1024,256]{1,0:T(8,128)(2,1)S(1)} %bitcast.36), channel_id=1, source_target_pairs={{0,6},{2,0},{4,2},{6,4},{1,7},{3,1},{5,3},{7,5},{8,14},{10,8},{12,... | collective-permute-start | bytes 1572872 | tf_op jit(solution)/shard_map/ppermute | solution.py:76
  27.3 38.9 %collective-permute-start.17 = (bf16[1024,256]{1,0:T(8,128)(2,1)S(1)}, bf16[1024,256]{1,0:T(8,128)(2,1)}, u32[]{:S(2)}, u32[]{:S(2)}) collective-permute-start(bf16[1024,256]{1,0:T(8,128)(2,1)S(1)} %bitcast.37), channel_id=1, source_target_pairs={{0,1},{1,0},{2,3},{3,2},{4,5},{5,4},{6,7},{7,6},{8,9},{9,8},{10,11... | collective-permute-start | bytes 1572872 | tf_op jit(solution)/shard_map/ppermute | solution.py:83
  37.5 15.0 %collective-permute-start.15 = (bf16[512,256]{1,0:T(8,128)(2,1)S(1)}, bf16[512,256]{1,0:T(8,128)(2,1)}, u32[]{:S(2)}, u32[]{:S(2)}) collective-permute-start(bf16[512,256]{1,0:T(8,128)(2,1)S(1)} %slice.38), channel_id=1, source_target_pairs={{0,2},{2,4},{4,6},{6,0},{1,3},{3,5},{5,7},{7,1},{8,10},{10,12},{12... | collective-permute-start | bytes 786440 | tf_op jit(solution)/shard_map/ppermute | solution.py:77
  37.6 28.6 %collective-permute-start.18 = (bf16[1024,256]{1,0:T(8,128)(2,1)S(1)}, bf16[1024,256]{1,0:T(8,128)(2,1)}, u32[]{:S(2)}, u32[]{:S(2)}) collective-permute-start(bf16[1024,256]{1,0:T(8,128)(2,1)S(1)} %collective-permute-done.13.refs_1_), channel_id=1, source_target_pairs={{0,1},{1,0},{2,3},{3,2},{4,5},{5,4},{6,7},{7,6},{8,9},{9,8},{10,11... | collective-permute-start | bytes 1572872 | tf_op jit(solution)/shard_map/ppermute | solution.py:83
  40.6 25.6 %collective-permute-start.19 = (bf16[1024,256]{1,0:T(8,128)(2,1)S(1)}, bf16[1024,256]{1,0:T(8,128)(2,1)}, u32[]{:S(2)}, u32[]{:S(2)}) collective-permute-start(bf16[1024,256]{1,0:T(8,128)(2,1)S(1)} %collective-permute-done.14.refs_2_), channel_id=1, source_target_pairs={{0,1},{1,0},{2,3},{3,2},{4,5},{5,4},{6,7},{7,6},{8,9},{9,8},{10,11... | collective-permute-start | bytes 1572872 | tf_op jit(solution)/shard_map/ppermute | solution.py:83
  40.7 12.9 %collective-permute-start.16 = (bf16[512,256]{1,0:T(8,128)(2,1)S(1)}, bf16[512,256]{1,0:T(8,128)(2,1)}, u32[]{:S(2)}, u32[]{:S(2)}) collective-permute-start(bf16[512,256]{1,0:T(8,128)(2,1)S(1)} %slice.39), channel_id=1, source_target_pairs={{0,6},{2,0},{4,2},{6,4},{1,7},{3,1},{5,3},{7,5},{8,14},{10,8},{12,... | collective-permute-start | bytes 786440 | tf_op jit(solution)/shard_map/ppermute | solution.py:78
  44.3 21.9 %all-to-all-start.1 = ((bf16[8,112,128]{2,1,0:T(8,128)(2,1)}), bf16[8,112,128]{2,1,0:T(8,128)(2,1)S(1)}, u32[]{:S(2)}, u32[]{:S(2)}) async-start(bf16[8,112,128]{2,1,0:T(8,128)(2,1)} %bitcast.11), calls=%async_computation.1 | async-start | bytes 458752 | tf_op jit(solution)/shard_map/all_to_all | solution.py:66
  52.5 121.3 %all-gather.5.cloned.1.call-start = ((), (), s32[]{:S(2)}) async-start(), calls=%async_computation.7 | async-start | bytes 4128768 | tf_op jit(solution)/shard_map/all_gather | solution.py:415
  52.5 13.7 %collective-permute-start.20 = (bf16[512,256]{1,0:T(8,128)(2,1)}, bf16[512,256]{1,0:T(8,128)(2,1)S(1)}, u32[]{:S(2)}, u32[]{:S(2)}) collective-permute-start(bf16[512,256]{1,0:T(8,128)(2,1)} %collective-permute-done.15.refs_3_), channel_id=1, source_target_pairs={{0,1},{1,0},{2,3},{3,2},{4,5},{5,4},{6,7},{7,6},{8,9},{9,8},{10,11... | collective-permute-start | bytes 786440 | tf_op jit(solution)/shard_map/ppermute | solution.py:83
  53.6 12.6 %collective-permute-start.21 = (bf16[512,256]{1,0:T(8,128)(2,1)}, bf16[512,256]{1,0:T(8,128)(2,1)S(1)}, u32[]{:S(2)}, u32[]{:S(2)}) collective-permute-start(bf16[512,256]{1,0:T(8,128)(2,1)} %collective-permute-done.16.refs_4_), channel_id=1, source_target_pairs={{0,1},{1,0},{2,3},{3,2},{4,5},{5,4},{6,7},{7,6},{8,9},{9,8},{10,11... | collective-permute-start | bytes 786440 | tf_op jit(solution)/shard_map/ppermute | solution.py:83
  71.5 12.1 %collective-permute-start.22 = (bf16[112,2048]{1,0:T(8,128)(2,1)}, bf16[112,2048]{1,0:T(8,128)(2,1)S(1)}, u32[]{:S(2)}, u32[]{:S(2)}) collective-permute-start(bf16[112,2048]{1,0:T(8,128)(2,1)} %shard_map.140.own), channel_id=1, source_target_pairs={{0,8},{8,16},{16,24},{24,0},{1,9},{9,17},{17,25},{25,1},{2,10},{10... | collective-permute-start | bytes 1376264 | tf_op jit(solution)/shard_map/ppermute | solution.py:75
  71.8 11.9 %collective-permute-start.23 = (bf16[112,2048]{1,0:T(8,128)(2,1)}, bf16[112,2048]{1,0:T(8,128)(2,1)S(1)}, u32[]{:S(2)}, u32[]{:S(2)}) collective-permute-start(bf16[112,2048]{1,0:T(8,128)(2,1)} %shard_map.140.own), channel_id=1, source_target_pairs={{0,24},{8,0},{16,8},{24,16},{1,25},{9,1},{17,9},{25,17},{2,26},{10... | collective-permute-start | bytes 1376264 | tf_op jit(solution)/shard_map/ppermute | solution.py:76
  98.2 23.1 %collective-permute-start.2 = (bf16[128,4096]{1,0:T(8,128)(2,1)}, bf16[128,4096]{1,0:T(8,128)(2,1)S(1)}, u32[]{:S(2)}, u32[]{:S(2)}) collective-permute-start(bf16[128,4096]{1,0:T(8,128)(2,1)} %get-tuple-element.18), channel_id=1, source_target_pairs={{0,8},{8,16},{16,24},{24,0},{1,9},{9,17},{17,25},{25,1},{2,10},{10... | collective-permute-start | bytes 3145736 | tf_op jit(solution)/shard_map/ppermute | solution.py:75
  98.2 27.2 %collective-permute-start = (bf16[128,4096]{1,0:T(8,128)(2,1)}, bf16[128,4096]{1,0:T(8,128)(2,1)S(1)}, u32[]{:S(2)}, u32[]{:S(2)}) collective-permute-start(bf16[128,4096]{1,0:T(8,128)(2,1)} %get-tuple-element.18), channel_id=1, source_target_pairs={{0,24},{8,0},{16,8},{24,16},{1,25},{9,1},{17,9},{25,17},{2,26},{10... | collective-permute-start | bytes 3145736 | tf_op jit(solution)/shard_map/ppermute | solution.py:76
  121.3 11.0 %collective-permute-start.4 = (bf16[64,4096]{1,0:T(8,128)(2,1)S(1)}, bf16[64,4096]{1,0:T(8,128)(2,1)S(1)}, u32[]{:S(2)}, u32[]{:S(2)}) collective-permute-start(bf16[64,4096]{1,0:T(8,128)(2,1)S(1)} %slice.36), channel_id=1, source_target_pairs={{0,8},{8,16},{16,24},{24,0},{1,9},{9,17},{17,25},{25,1},{2,10},{10... | collective-permute-start | bytes 1572872 | tf_op jit(solution)/shard_map/ppermute | solution.py:77
  121.4 19.2 %collective-permute-start.3 = (bf16[128,4096]{1,0:T(8,128)(2,1)S(1)}, bf16[128,4096]{1,0:T(8,128)(2,1)S(1)}, u32[]{:S(2)}, u32[]{:S(2)}) collective-permute-start(bf16[128,4096]{1,0:T(8,128)(2,1)S(1)} %collective-permute-done.2.refs_3_), channel_id=1, source_target_pairs={{0,1},{1,0},{2,3},{3,2},{4,5},{5,4},{6,7},{7,6},{8,9},{9,8},{10,11... | collective-permute-start | bytes 3145736 | tf_op jit(solution)/shard_map/ppermute | solution.py:83
  125.4 15.2 %collective-permute-start.1 = (bf16[128,4096]{1,0:T(8,128)(2,1)S(1)}, bf16[128,4096]{1,0:T(8,128)(2,1)S(1)}, u32[]{:S(2)}, u32[]{:S(2)}) collective-permute-start(bf16[128,4096]{1,0:T(8,128)(2,1)S(1)} %collective-permute-done.refs_1_), channel_id=1, source_target_pairs={{0,1},{1,0},{2,3},{3,2},{4,5},{5,4},{6,7},{7,6},{8,9},{9,8},{10,11... | collective-permute-start | bytes 3145736 | tf_op jit(solution)/shard_map/ppermute | solution.py:83
  125.6 13.8 %collective-permute-start.5 = (bf16[64,4096]{1,0:T(8,128)(2,1)S(1)}, bf16[64,4096]{1,0:T(8,128)(2,1)S(1)}, u32[]{:S(2)}, u32[]{:S(2)}) collective-permute-start(bf16[64,4096]{1,0:T(8,128)(2,1)S(1)} %slice.37), channel_id=1, source_target_pairs={{0,24},{8,0},{16,8},{24,16},{1,25},{9,1},{17,9},{25,17},{2,26},{10... | collective-permute-start | bytes 1572872 | tf_op jit(solution)/shard_map/ppermute | solution.py:78
  180.7 23.7 %all-to-all-start.2 = ((bf16[8,320,256]{2,1,0:T(8,128)(2,1)}), bf16[8,320,256]{2,1,0:T(8,128)(2,1)S(1)}, u32[]{:S(2)}, u32[]{:S(2)}) async-start(bf16[8,320,256]{2,1,0:T(8,128)(2,1)} %shard_map.142), calls=%async_computation.2 | async-start | bytes 2621440 | tf_op jit(solution)/shard_map/all_to_all | solution.py:66
  206.9 54.2 %all-to-all-start.4 = ((bf16[8,256,1024]{2,1,0:T(8,128)(2,1)}), bf16[8,256,1024]{2,1,0:T(8,128)(2,1)}, u32[]{:S(2)}, u32[]{:S(2)}) async-start(bf16[8,256,1024]{2,1,0:T(8,128)(2,1)} %broadcast_in_dim.2), calls=%async_computation.4 | async-start | bytes 8388608 | tf_op jit(solution)/shard_map/all_to_all | solution.py:66
  223.8 18.8 %collective-permute-start.26 = (f32[32,256]{1,0:T(8,128)S(1)}, f32[32,256]{1,0:T(8,128)S(1)}, u32[]{:S(2)}, u32[]{:S(2)}) collective-permute-start(f32[32,256]{1,0:T(8,128)S(1)} %get-tuple-element.28), channel_id=1, source_target_pairs={{0,8},{8,16},{16,24},{24,32},{32,40},{40,48},{48,56},{56,64},{64,7... | collective-permute-start | bytes 98312 | tf_op jit(solution)/shard_map/ppermute | solution.py:423
  226.7 15.8 %collective-permute-start.27 = (f32[32,256]{1,0:T(8,128)S(1)}, f32[32,256]{1,0:T(8,128)S(1)}, u32[]{:S(2)}, u32[]{:S(2)}) collective-permute-start(f32[32,256]{1,0:T(8,128)S(1)} %get-tuple-element.27), channel_id=1, source_target_pairs={{8,0},{16,8},{24,16},{32,24},{40,32},{48,40},{56,48},{64,56},{72,6... | collective-permute-start | bytes 98312 | tf_op jit(solution)/shard_map/ppermute | solution.py:424
  (42 other events, 312.8 us)
Sparse Core Ops, SparseCore 0:
  23.5 61.5 all-gather.2
  93.7 46.3 all-gather.4

commit v4 on v3

--- a/solution.py
+++ b/solution.py
@@ -274,20 +274,23 @@
         out[f] = total.astype(BF)
         return carry
 
-    lax.fori_loop(0, NF, body, 0)
-
-
-def keys_kernel(parts, own, above, below, kv):
-    total = jnp.concatenate([above[...], own[...], below[...]], axis=0)
-    for i in range(NF):
-        total = total + parts[i].astype(F32)
-    kv[...] = total.astype(BF)
-
-
-def cross_kernel(place, query, byte_patch, stacked, context_s, out):
+    lax.fori_loop(0, NF, body, 0, unroll=True)
+
+
+def cross_kernel(
+    place, query, byte_patch, parts, own, above, below, context_s, out, stacked
+):
     total, both = stacked.shape
     cols = both // 2
-    rows = total - 2 * HALO
+    rows = own.shape[0]
+
+    @pl.when(pl.program_id(0) == 0)
+    def _():
+        sums = jnp.concatenate([above[...], own[...], below[...]], axis=0)
+        for i in range(NF):
+            sums = sums + parts[i].astype(F32)
+        stacked[...] = sums.astype(BF)
+
     shape = (total, query.shape[0])
     index = lax.broadcasted_iota(jnp.int32, shape, 0) + (place[3] * rows - HALO)
     held = byte_patch[...]
@@ -308,8 +311,12 @@
     out[:, cols:] = context_s[...]
 
 
-def cross_attention(place, query, byte_patch, kv, context_s):
+def cross_attention(place, query, byte_patch, parts, own, above, below, context_s):
     count, cols = query.shape
+
+    def whole(value):
+        return pl.BlockSpec(value.shape, lambda i: (0,) * value.ndim)
+
     block = pl.BlockSpec((BROWS, cols), lambda i: (i, 0))
     return pl.pallas_call(
         cross_kernel,
@@ -319,12 +326,16 @@
             pl.BlockSpec(memory_space=pltpu.SMEM),
             block,
             pl.BlockSpec((1, BROWS), lambda i: (0, i)),
-            pl.BlockSpec(kv.shape, lambda i: (0, 0)),
+            whole(parts),
+            whole(own),
+            whole(above),
+            whole(below),
             block,
         ],
         out_specs=pl.BlockSpec((BROWS, 2 * cols), lambda i: (i, 0)),
-        cost_estimate=cost(6),
-    )(place, query, byte_patch.reshape(1, count), kv, context_s)
+        scratch_shapes=[pltpu.VMEM(parts.shape[1:], BF)],
+        cost_estimate=cost(8),
+    )(place, query, byte_patch.reshape(1, count), parts, own, above, below, context_s)
 
 
 def update_kernel(context, outs, out):
@@ -464,16 +475,9 @@
         scratch=(pltpu.VMEM((NY, rows + 2 * HALO, slot), BF),),
     )
     part = swap(part, FFN)
-    both_c = call(
-        keys_kernel,
-        sds((rows + 2 * HALO, both_cols), BF),
-        part,
-        own_kv,
-        own_above,
-        own_below,
-    )
-
-    context = cross_attention(place, query_c, byte_patch, both_c, context_s)
+    context = cross_attention(
+        place, query_c, byte_patch, part, own_kv, own_above, own_below, context_s
+    )
     context = swap(context.reshape(NF, chunk, both_cols), FFN)
     update = call(update_kernel, sds((NF, chunk, head_cols), BF), context, outs)
     return swap(update, FFN).reshape(byte_count, head_cols)

time: 310 us -> 308 us (level)
    pallas_call x8 -> x7, Pallas kernels: 35.2 us -> 31.6 us  [call(): pl.pallas_call(kernel, out_shape=out, in_specs=specs, out_specs=jax.tree....]
where the time goes in v4:
time: 308 us; the launch traced here: 306 us
  waiting for transfers between devices  100 us (32%)
  starting transfers between devices  67.4 us (22%)
  Pallas kernels  57.6 us (19%)
  blocking collectives  47.3 us (15%)
  local copies, waits for them, and re-layouts  16.7 us (5%)
  between operations  13.8 us (4%)
    all_to_all x3, blocking collectives, swap(): return lax.all_to_all(value, axes, split_axis=0, concat_axis=0, tiled=True)  47.3 us
    all_to_all x3, waiting for transfers between devices, swap(): return lax.all_to_all(value, axes, split_axis=0, concat_axis=0, tiled=True)  40.6 us
    ppermute x3, waiting for transfers between devices, ring(): before = lax.ppermute(value, axis, UP)  37.6 us
    pallas_call x7, Pallas kernels, call(): pl.pallas_call(kernel, out_shape=out, in_specs=specs, out_specs=jax.tree....  31.6 us
    all_to_all x3, starting transfers between devices, swap(): return lax.all_to_all(value, axes, split_axis=0, concat_axis=0, tiled=True)  19.5 us
    ppermute x9, starting transfers between devices, other_core(): return lax.ppermute(value, 'c', [(0, 1), (1, 0)])  16.6 us
    pallas_call x1, Pallas kernels, window_attention(): pl.pallas_call(window_kernel, out_shape=sds((count, cols), BF), grid=(cou...  12.8 us
    unnamed x68, local copies, waits for them, and re-layouts  11.1 us
  transfers between devices with their start and end apart: 34, of which 14 were waited for; matrix products, arithmetic and copies ran while one was open for 2% of the time, Pallas kernels for 16%

profile of v4, /device:TPU:1, one launch (start us, length us, event | category | flops | bytes accessed | tf_op | source)
XLA Modules:
  0.0 305.9 jit_solution(2803795808348817853)
XLA Ops:
  8.9 13.4 %all_to_all.30 = bf16[4,128,512]{1,2,0:T(8,128)(2,1)S(1)} all-to-all(bf16[4,128,512]{1,2,0:T(8,128)(2,1)S(1)} %fusion.2), channel_id=1, replica_groups=mesh['z'=8,'y'=4,'x'=4,'c'=2] {'y'}, dimensions={0} | all-to-all | bytes 1048576 | tf_op jit(solution)/shard_map/all_to_all | solution.py:66
  29.7 7.8 %collective-permute-done.13.refs_1_ = bf16[1024,256]{1,0:T(8,128)(2,1)S(1)} collective-permute-done((bf16[1024,256]{1,0:T(8,128)(2,1)S(1)}, bf16[1024,256]{1,0:T(8,128)(2,1)S(1)}, u32[]{:S(2)}, u32[]{:S(2)}) %collective-permute-start.13) | collective-permute-done | bytes 524320 | tf_op jit(solution)/shard_map/ppermute | solution.py:75
  44.3 8.2 %all-to-all-start.1 = ((bf16[8,112,128]{2,1,0:T(8,128)(2,1)}), bf16[8,112,128]{2,1,0:T(8,128)(2,1)S(1)}, u32[]{:S(2)}, u32[]{:S(2)}) async-start(bf16[8,112,128]{2,1,0:T(8,128)(2,1)} %bitcast.11), calls=%async_computation.1 | async-start | bytes 458752 | tf_op jit(solution)/shard_map/all_to_all | solution.py:66
  54.4 11.8 %all-to-all-done.1.down_t = bf16[8,112,128]{2,1,0:T(8,128)(2,1)S(1)} async-done(((bf16[8,112,128]{2,1,0:T(8,128)(2,1)}), bf16[8,112,128]{2,1,0:T(8,128)(2,1)S(1)}, u32[]{:S(2)}, u32[]{:S(2)}) %all-to-all-start.1) | async-done | bytes 229408 | tf_op jit(solution)/shard_map/all_to_all | solution.py:66
  67.7 3.8 %shard_map.140.own = bf16[112,2048]{1,0:T(8,128)(2,1)} custom-call(s32[4]{0:T(128)} %pad_add_fusion.place, bf16[8,112,128]{2,1,0:T(8,128)(2,1)} %copy-done.15, bf16[1024,256]{1,0:T(8,128)(2,1)} %bitcast.38, bf16[1024,256]{1,0:T(8,128)(2,1)} %copy-done.17, bf16[1024,256]{1,0:T(8,128)(2,1)} %copy-done.18, bf16[512,256]{1,0:T(8,128)(2,1)} %collective-permute-done.15.refs_3_, ...), custom_call_target="tpu_custom_call" | custom-call | flops 2400000000 | bytes 10000000 | tf_op jit(solution)/shard_map/pallas_call | solution.py:55
  74.2 9.4 %collective-permute-done.22.before = bf16[112,2048]{1,0:T(8,128)(2,1)S(1)} collective-permute-done((bf16[112,2048]{1,0:T(8,128)(2,1)}, bf16[112,2048]{1,0:T(8,128)(2,1)S(1)}, u32[]{:S(2)}, u32[]{:S(2)}) %collective-permute-start.22) | collective-permute-done | bytes 458784 | tf_op jit(solution)/shard_map/ppermute | solution.py:75
  93.6 4.6 %shard_map.137 = (bf16[256,4096]{1,0:T(8,128)(2,1)}, bf16[128,4096]{1,0:T(8,128)(2,1)}) custom-call(s32[4]{0:T(128)} %pad_add_fusion.place, bf16[256,4096]{1,0:T(8,128)(2,1)} %patches.1), custom_call_target="tpu_custom_call" | custom-call | flops 2400000000 | bytes 10000000 | tf_op jit(solution)/shard_map/pallas_call | solution.py:55
  100.9 20.4 %collective-permute-done.2.refs_3_ = bf16[128,4096]{1,0:T(8,128)(2,1)S(1)} collective-permute-done((bf16[128,4096]{1,0:T(8,128)(2,1)}, bf16[128,4096]{1,0:T(8,128)(2,1)S(1)}, u32[]{:S(2)}, u32[]{:S(2)}) %collective-permute-start.2) | collective-permute-done | bytes 1048608 | tf_op jit(solution)/shard_map/ppermute | solution.py:75
  121.4 4.0 %collective-permute-start.3 = (bf16[128,4096]{1,0:T(8,128)(2,1)S(1)}, bf16[128,4096]{1,0:T(8,128)(2,1)S(1)}, u32[]{:S(2)}, u32[]{:S(2)}) collective-permute-start(bf16[128,4096]{1,0:T(8,128)(2,1)S(1)} %collective-permute-done.2.refs_3_), channel_id=1, source_target_pairs={{0,1},{1,0},{2,3},{3,2},{4,5},{5,4},{6,7},{7,6},{8,9},{9,8},{10,11... | collective-permute-start | bytes 3145736 | tf_op jit(solution)/shard_map/ppermute | solution.py:83
  128.5 3.8 %collective-permute-done.4.refs_5_ = bf16[64,4096]{1,0:T(8,128)(2,1)S(1)} collective-permute-done((bf16[64,4096]{1,0:T(8,128)(2,1)S(1)}, bf16[64,4096]{1,0:T(8,128)(2,1)S(1)}, u32[]{:S(2)}, u32[]{:S(2)}) %collective-permute-start.4) | collective-permute-done | bytes 524320 | tf_op jit(solution)/shard_map/ppermute | solution.py:77
  132.3 4.7 %collective-permute-start.6 = (bf16[64,4096]{1,0:T(8,128)(2,1)S(1)}, bf16[64,4096]{1,0:T(8,128)(2,1)S(1)}, u32[]{:S(2)}, u32[]{:S(2)}) collective-permute-start(bf16[64,4096]{1,0:T(8,128)(2,1)S(1)} %collective-permute-done.4.refs_5_), channel_id=1, source_target_pairs={{0,1},{1,0},{2,3},{3,2},{4,5},{5,4},{6,7},{7,6},{8,9},{9,8},{10,11... | collective-permute-start | bytes 1572872 | tf_op jit(solution)/shard_map/ppermute | solution.py:83
  142.8 9.5 %shard_map.138 = (bf16[256,256]{1,0:T(8,128)(2,1)}, bf16[256,256]{1,0:T(8,128)(2,1)}, bf16[256,256]{1,0:T(8,128)(2,1)}, bf16[256,256]{1,0:T(8,128)(2,1)}) custom-call(s32[4]{0:T(128)} %pad_add_fusion.place, bf16[256,4096]{1,0:T(8,128)(2,1)} %get-tuple-element.17.refs_0_, bf16[128,4096]{1,0:T(8,128)(2,1)} %copy-done.2, bf16[128,4096]{1,0:T(8,128)(2,1)} %copy-done.7, ...), custom_call_target="tpu_custom_call" | custom-call | flops 2400000000 | bytes 10000000 | tf_op jit(solution)/shard_map/pallas_call | solution.py:55
  158.7 6.0 %collective-permute-done.9.before = bf16[256,256]{1,0:T(8,128)(2,1)S(1)} collective-permute-done((bf16[256,256]{1,0:T(8,128)(2,1)}, bf16[256,256]{1,0:T(8,128)(2,1)S(1)}, u32[]{:S(2)}, u32[]{:S(2)}) %collective-permute-start.9) | collective-permute-done | bytes 131104 | tf_op jit(solution)/shard_map/ppermute | solution.py:456
  174.4 5.0 %shard_map.142 = bf16[8,320,256]{2,1,0:T(8,128)(2,1)} custom-call(s32[4]{0:T(128)} %pad_add_fusion.place, bf16[256,256]{1,0:T(8,128)(2,1)} %get-tuple-element.19.own, bf16[256,256]{1,0:T(8,128)(2,1)} %copy-done.25, bf16[256,256]{1,0:T(8,128)(2,1)} %copy-done.26, bf16[256,256]{1,0:T(8,128)(2,1)} %copy-done.27, bf16[4,32,256]{2,1,0:T(8,128)(2,1)} %copy-done.28, ...), custom_call_target="tpu_custom_call" | custom-call | flops 2400000000 | bytes 10000000 | tf_op jit(solution)/shard_map/pallas_call | solution.py:55
  179.3 5.9 %all-to-all-start.2 = ((bf16[8,320,256]{2,1,0:T(8,128)(2,1)}), bf16[8,320,256]{2,1,0:T(8,128)(2,1)S(1)}, u32[]{:S(2)}, u32[]{:S(2)}) async-start(bf16[8,320,256]{2,1,0:T(8,128)(2,1)} %shard_map.142), calls=%async_computation.2 | async-start | bytes 2621440 | tf_op jit(solution)/shard_map/all_to_all | solution.py:66
  185.3 17.8 %all-to-all-done.2.parts = bf16[8,320,256]{2,1,0:T(8,128)(2,1)S(1)} async-done(((bf16[8,320,256]{2,1,0:T(8,128)(2,1)}), bf16[8,320,256]{2,1,0:T(8,128)(2,1)S(1)}, u32[]{:S(2)}, u32[]{:S(2)}) %all-to-all-start.2) | async-done | bytes 1310752 | tf_op jit(solution)/shard_map/all_to_all | solution.py:66
  205.6 5.4 %all-to-all-start.4 = ((bf16[8,256,1024]{2,1,0:T(8,128)(2,1)}), bf16[8,256,1024]{2,1,0:T(8,128)(2,1)}, u32[]{:S(2)}, u32[]{:S(2)}) async-start(bf16[8,256,1024]{2,1,0:T(8,128)(2,1)} %broadcast_in_dim.2), calls=%async_computation.4 | async-start | bytes 8388608 | tf_op jit(solution)/shard_map/all_to_all | solution.py:66
  211.1 6.1 %shard_map.136 = (bf16[2048,128]{1,0:T(8,128)(2,1)}, bf16[2048,128]{1,0:T(8,128)(2,1)}, bf16[2048,256]{1,0:T(8,128)(2,1)}) custom-call(bf16[2048,1024]{1,0:T(8,128)(2,1)} %states.1, bf16[1024,128]{1,0:T(8,128)(2,1)} %w_qs.1, bf16[1024,128]{1,0:T(8,128)(2,1)} %w_qc.1, bf16[1024,128]{1,0:T(8,128)(2,1)} %w_k.1, bf16[1024,128]{1,0:T(8,128)(2,1)} %w_v.1), custom_call_target="tpu_custom_call" | custom-call | flops 3600000000 | bytes 15000000 | tf_op jit(solution)/shard_map/pallas_call | solution.py:148
  228.4 12.8 %shard_map.143.context_s = bf16[2048,128]{1,0:T(8,128)(2,1)} custom-call(s32[4]{0:T(128)} %pad_add_fusion.place, bf16[2048,128]{1,0:T(8,128)(2,1)} %get-tuple-element.25.query, bf16[2048,256]{1,0:T(8,128)(2,1)} %get-tuple-element.26.kv, bf16[512,256]{1,0:T(8,128)(2,1)} %copy-done.22), custom_call_target="tpu_custom_call" | custom-call | flops 8400000000 | bytes 35000000 | tf_op jit(solution)/shard_map/pallas_call | solution.py:199
  241.8 7.0 %shard_map.144 = bf16[2048,256]{1,0:T(8,128)(2,1)} custom-call(s32[4]{0:T(128)} %pad_add_fusion.place, bf16[2048,128]{1,0:T(8,128)(2,1)} %get-tuple-element.16.query, s32[1,2048]{1,0:T(1,128)} %bitcast.40, bf16[8,320,256]{2,1,0:T(8,128)(2,1)} %copy-done.5, f32[256,256]{1,0:T(8,128)} %pad_maximum_fusion.2.own, f32[32,256]{1,0:T(8,128)} %copy-done.30, ...), custom_call_target="tpu_custom_call" | custom-call | flops 4800000000 | bytes 20000000 | tf_op jit(solution)/shard_map/pallas_call | solution.py:321
  248.9 11.0 %all-to-all-done.4 = bf16[8,256,1024]{2,1,0:T(8,128)(2,1)} async-done(((bf16[8,256,1024]{2,1,0:T(8,128)(2,1)}), bf16[8,256,1024]{2,1,0:T(8,128)(2,1)}, u32[]{:S(2)}, u32[]{:S(2)}) %all-to-all-start.4) | async-done | bytes 4194336 | tf_op jit(solution)/shard_map/all_to_all | solution.py:66
  259.9 20.1 %all_to_all.31.context = bf16[8,256,256]{2,1,0:T(8,128)(2,1)} all-to-all(bf16[8,256,256]{2,1,0:T(8,128)(2,1)} %bitcast.32), channel_id=1, replica_groups=mesh['z'=8,'y'=4,'x'=4,'c'=2] {'x','c'}, dimensions={0} | all-to-all | bytes 2097152 | tf_op jit(solution)/shard_map/all_to_all | solution.py:66
  280.0 4.6 %shard_map.145 = bf16[8,256,128]{2,1,0:T(8,128)(2,1)} custom-call(bf16[8,256,256]{2,1,0:T(8,128)(2,1)} %all_to_all.31.context, bf16[2048,1024]{1,0:T(8,128)(2,1)} %bitcast.16.outs), custom_call_target="tpu_custom_call" | custom-call | flops 2400000000 | bytes 10000000 | tf_op jit(solution)/shard_map/pallas_call | solution.py:55
  284.6 13.8 %all_to_all.32 = bf16[8,256,128]{2,1,0:T(8,128)(2,1)S(1)} all-to-all(bf16[8,256,128]{2,1,0:T(8,128)(2,1)} %shard_map.145), channel_id=1, replica_groups=mesh['z'=8,'y'=4,'x'=4,'c'=2] {'x','c'}, dimensions={0} | all-to-all | bytes 1048576 | tf_op jit(solution)/shard_map/all_to_all | solution.py:66
  (145 shorter events, 75.2 us)
Async XLA Ops:
  6.5 136.2 %all-gather.3.cloned.1.call-start = ((), (), s32[]{:S(2)}) async-start(), calls=%async_computation.6 | async-start | bytes 4718592 | tf_op jit(solution)/shard_map/all_gather | solution.py:401
  24.5 13.0 %collective-permute-start.13 = (bf16[1024,256]{1,0:T(8,128)(2,1)S(1)}, bf16[1024,256]{1,0:T(8,128)(2,1)S(1)}, u32[]{:S(2)}, u32[]{:S(2)}) collective-permute-start(bf16[1024,256]{1,0:T(8,128)(2,1)S(1)} %bitcast.35), channel_id=1, source_target_pairs={{0,2},{2,4},{4,6},{6,0},{1,3},{3,5},{5,7},{7,1},{8,10},{10,12},{12... | collective-permute-start | bytes 1572872 | tf_op jit(solution)/shard_map/ppermute | solution.py:75
  25.8 14.7 %collective-permute-start.14 = (bf16[1024,256]{1,0:T(8,128)(2,1)S(1)}, bf16[1024,256]{1,0:T(8,128)(2,1)S(1)}, u32[]{:S(2)}, u32[]{:S(2)}) collective-permute-start(bf16[1024,256]{1,0:T(8,128)(2,1)S(1)} %bitcast.36), channel_id=1, source_target_pairs={{0,6},{2,0},{4,2},{6,4},{1,7},{3,1},{5,3},{7,5},{8,14},{10,8},{12,... | collective-permute-start | bytes 1572872 | tf_op jit(solution)/shard_map/ppermute | solution.py:76
  27.3 38.9 %collective-permute-start.17 = (bf16[1024,256]{1,0:T(8,128)(2,1)S(1)}, bf16[1024,256]{1,0:T(8,128)(2,1)}, u32[]{:S(2)}, u32[]{:S(2)}) collective-permute-start(bf16[1024,256]{1,0:T(8,128)(2,1)S(1)} %bitcast.37), channel_id=1, source_target_pairs={{0,1},{1,0},{2,3},{3,2},{4,5},{5,4},{6,7},{7,6},{8,9},{9,8},{10,11... | collective-permute-start | bytes 1572872 | tf_op jit(solution)/shard_map/ppermute | solution.py:83
  37.5 15.0 %collective-permute-start.15 = (bf16[512,256]{1,0:T(8,128)(2,1)S(1)}, bf16[512,256]{1,0:T(8,128)(2,1)}, u32[]{:S(2)}, u32[]{:S(2)}) collective-permute-start(bf16[512,256]{1,0:T(8,128)(2,1)S(1)} %slice.38), channel_id=1, source_target_pairs={{0,2},{2,4},{4,6},{6,0},{1,3},{3,5},{5,7},{7,1},{8,10},{10,12},{12... | collective-permute-start | bytes 786440 | tf_op jit(solution)/shard_map/ppermute | solution.py:77
  37.6 28.6 %collective-permute-start.18 = (bf16[1024,256]{1,0:T(8,128)(2,1)S(1)}, bf16[1024,256]{1,0:T(8,128)(2,1)}, u32[]{:S(2)}, u32[]{:S(2)}) collective-permute-start(bf16[1024,256]{1,0:T(8,128)(2,1)S(1)} %collective-permute-done.13.refs_1_), channel_id=1, source_target_pairs={{0,1},{1,0},{2,3},{3,2},{4,5},{5,4},{6,7},{7,6},{8,9},{9,8},{10,11... | collective-permute-start | bytes 1572872 | tf_op jit(solution)/shard_map/ppermute | solution.py:83
  40.6 25.6 %collective-permute-start.19 = (bf16[1024,256]{1,0:T(8,128)(2,1)S(1)}, bf16[1024,256]{1,0:T(8,128)(2,1)}, u32[]{:S(2)}, u32[]{:S(2)}) collective-permute-start(bf16[1024,256]{1,0:T(8,128)(2,1)S(1)} %collective-permute-done.14.refs_2_), channel_id=1, source_target_pairs={{0,1},{1,0},{2,3},{3,2},{4,5},{5,4},{6,7},{7,6},{8,9},{9,8},{10,11... | collective-permute-start | bytes 1572872 | tf_op jit(solution)/shard_map/ppermute | solution.py:83
  40.7 12.9 %collective-permute-start.16 = (bf16[512,256]{1,0:T(8,128)(2,1)S(1)}, bf16[512,256]{1,0:T(8,128)(2,1)}, u32[]{:S(2)}, u32[]{:S(2)}) collective-permute-start(bf16[512,256]{1,0:T(8,128)(2,1)S(1)} %slice.39), channel_id=1, source_target_pairs={{0,6},{2,0},{4,2},{6,4},{1,7},{3,1},{5,3},{7,5},{8,14},{10,8},{12,... | collective-permute-start | bytes 786440 | tf_op jit(solution)/shard_map/ppermute | solution.py:78
  44.3 21.9 %all-to-all-start.1 = ((bf16[8,112,128]{2,1,0:T(8,128)(2,1)}), bf16[8,112,128]{2,1,0:T(8,128)(2,1)S(1)}, u32[]{:S(2)}, u32[]{:S(2)}) async-start(bf16[8,112,128]{2,1,0:T(8,128)(2,1)} %bitcast.11), calls=%async_computation.1 | async-start | bytes 458752 | tf_op jit(solution)/shard_map/all_to_all | solution.py:66
  52.5 121.3 %all-gather.5.cloned.1.call-start = ((), (), s32[]{:S(2)}) async-start(), calls=%async_computation.7 | async-start | bytes 4128768 | tf_op jit(solution)/shard_map/all_gather | solution.py:426
  52.5 13.7 %collective-permute-start.20 = (bf16[512,256]{1,0:T(8,128)(2,1)}, bf16[512,256]{1,0:T(8,128)(2,1)S(1)}, u32[]{:S(2)}, u32[]{:S(2)}) collective-permute-start(bf16[512,256]{1,0:T(8,128)(2,1)} %collective-permute-done.15.refs_3_), channel_id=1, source_target_pairs={{0,1},{1,0},{2,3},{3,2},{4,5},{5,4},{6,7},{7,6},{8,9},{9,8},{10,11... | collective-permute-start | bytes 786440 | tf_op jit(solution)/shard_map/ppermute | solution.py:83
  53.6 12.6 %collective-permute-start.21 = (bf16[512,256]{1,0:T(8,128)(2,1)}, bf16[512,256]{1,0:T(8,128)(2,1)S(1)}, u32[]{:S(2)}, u32[]{:S(2)}) collective-permute-start(bf16[512,256]{1,0:T(8,128)(2,1)} %collective-permute-done.16.refs_4_), channel_id=1, source_target_pairs={{0,1},{1,0},{2,3},{3,2},{4,5},{5,4},{6,7},{7,6},{8,9},{9,8},{10,11... | collective-permute-start | bytes 786440 | tf_op jit(solution)/shard_map/ppermute | solution.py:83
  71.5 12.1 %collective-permute-start.22 = (bf16[112,2048]{1,0:T(8,128)(2,1)}, bf16[112,2048]{1,0:T(8,128)(2,1)S(1)}, u32[]{:S(2)}, u32[]{:S(2)}) collective-permute-start(bf16[112,2048]{1,0:T(8,128)(2,1)} %shard_map.140.own), channel_id=1, source_target_pairs={{0,8},{8,16},{16,24},{24,0},{1,9},{9,17},{17,25},{25,1},{2,10},{10... | collective-permute-start | bytes 1376264 | tf_op jit(solution)/shard_map/ppermute | solution.py:75
  71.8 11.9 %collective-permute-start.23 = (bf16[112,2048]{1,0:T(8,128)(2,1)}, bf16[112,2048]{1,0:T(8,128)(2,1)S(1)}, u32[]{:S(2)}, u32[]{:S(2)}) collective-permute-start(bf16[112,2048]{1,0:T(8,128)(2,1)} %shard_map.140.own), channel_id=1, source_target_pairs={{0,24},{8,0},{16,8},{24,16},{1,25},{9,1},{17,9},{25,17},{2,26},{10... | collective-permute-start | bytes 1376264 | tf_op jit(solution)/shard_map/ppermute | solution.py:76
  98.2 23.1 %collective-permute-start.2 = (bf16[128,4096]{1,0:T(8,128)(2,1)}, bf16[128,4096]{1,0:T(8,128)(2,1)S(1)}, u32[]{:S(2)}, u32[]{:S(2)}) collective-permute-start(bf16[128,4096]{1,0:T(8,128)(2,1)} %get-tuple-element.18), channel_id=1, source_target_pairs={{0,8},{8,16},{16,24},{24,0},{1,9},{9,17},{17,25},{25,1},{2,10},{10... | collective-permute-start | bytes 3145736 | tf_op jit(solution)/shard_map/ppermute | solution.py:75
  98.2 27.2 %collective-permute-start = (bf16[128,4096]{1,0:T(8,128)(2,1)}, bf16[128,4096]{1,0:T(8,128)(2,1)S(1)}, u32[]{:S(2)}, u32[]{:S(2)}) collective-permute-start(bf16[128,4096]{1,0:T(8,128)(2,1)} %get-tuple-element.18), channel_id=1, source_target_pairs={{0,24},{8,0},{16,8},{24,16},{1,25},{9,1},{17,9},{25,17},{2,26},{10... | collective-permute-start | bytes 3145736 | tf_op jit(solution)/shard_map/ppermute | solution.py:76
  121.3 11.0 %collective-permute-start.4 = (bf16[64,4096]{1,0:T(8,128)(2,1)S(1)}, bf16[64,4096]{1,0:T(8,128)(2,1)S(1)}, u32[]{:S(2)}, u32[]{:S(2)}) collective-permute-start(bf16[64,4096]{1,0:T(8,128)(2,1)S(1)} %slice.36), channel_id=1, source_target_pairs={{0,8},{8,16},{16,24},{24,0},{1,9},{9,17},{17,25},{25,1},{2,10},{10... | collective-permute-start | bytes 1572872 | tf_op jit(solution)/shard_map/ppermute | solution.py:77
  121.4 19.2 %collective-permute-start.3 = (bf16[128,4096]{1,0:T(8,128)(2,1)S(1)}, bf16[128,4096]{1,0:T(8,128)(2,1)S(1)}, u32[]{:S(2)}, u32[]{:S(2)}) collective-permute-start(bf16[128,4096]{1,0:T(8,128)(2,1)S(1)} %collective-permute-done.2.refs_3_), channel_id=1, source_target_pairs={{0,1},{1,0},{2,3},{3,2},{4,5},{5,4},{6,7},{7,6},{8,9},{9,8},{10,11... | collective-permute-start | bytes 3145736 | tf_op jit(solution)/shard_map/ppermute | solution.py:83
  125.4 15.2 %collective-permute-start.1 = (bf16[128,4096]{1,0:T(8,128)(2,1)S(1)}, bf16[128,4096]{1,0:T(8,128)(2,1)S(1)}, u32[]{:S(2)}, u32[]{:S(2)}) collective-permute-start(bf16[128,4096]{1,0:T(8,128)(2,1)S(1)} %collective-permute-done.refs_1_), channel_id=1, source_target_pairs={{0,1},{1,0},{2,3},{3,2},{4,5},{5,4},{6,7},{7,6},{8,9},{9,8},{10,11... | collective-permute-start | bytes 3145736 | tf_op jit(solution)/shard_map/ppermute | solution.py:83
  125.6 13.8 %collective-permute-start.5 = (bf16[64,4096]{1,0:T(8,128)(2,1)S(1)}, bf16[64,4096]{1,0:T(8,128)(2,1)S(1)}, u32[]{:S(2)}, u32[]{:S(2)}) collective-permute-start(bf16[64,4096]{1,0:T(8,128)(2,1)S(1)} %slice.37), channel_id=1, source_target_pairs={{0,24},{8,0},{16,8},{24,16},{1,25},{9,1},{17,9},{25,17},{2,26},{10... | collective-permute-start | bytes 1572872 | tf_op jit(solution)/shard_map/ppermute | solution.py:78
  179.3 23.7 %all-to-all-start.2 = ((bf16[8,320,256]{2,1,0:T(8,128)(2,1)}), bf16[8,320,256]{2,1,0:T(8,128)(2,1)S(1)}, u32[]{:S(2)}, u32[]{:S(2)}) async-start(bf16[8,320,256]{2,1,0:T(8,128)(2,1)} %shard_map.142), calls=%async_computation.2 | async-start | bytes 2621440 | tf_op jit(solution)/shard_map/all_to_all | solution.py:66
  205.6 54.2 %all-to-all-start.4 = ((bf16[8,256,1024]{2,1,0:T(8,128)(2,1)}), bf16[8,256,1024]{2,1,0:T(8,128)(2,1)}, u32[]{:S(2)}, u32[]{:S(2)}) async-start(bf16[8,256,1024]{2,1,0:T(8,128)(2,1)} %broadcast_in_dim.2), calls=%async_computation.4 | async-start | bytes 8388608 | tf_op jit(solution)/shard_map/all_to_all | solution.py:66
  222.4 18.8 %collective-permute-start.26 = (f32[32,256]{1,0:T(8,128)S(1)}, f32[32,256]{1,0:T(8,128)S(1)}, u32[]{:S(2)}, u32[]{:S(2)}) collective-permute-start(f32[32,256]{1,0:T(8,128)S(1)} %get-tuple-element.28), channel_id=1, source_target_pairs={{0,8},{8,16},{16,24},{24,32},{32,40},{40,48},{48,56},{56,64},{64,7... | collective-permute-start | bytes 98312 | tf_op jit(solution)/shard_map/ppermute | solution.py:434
  225.4 15.8 %collective-permute-start.27 = (f32[32,256]{1,0:T(8,128)S(1)}, f32[32,256]{1,0:T(8,128)S(1)}, u32[]{:S(2)}, u32[]{:S(2)}) collective-permute-start(f32[32,256]{1,0:T(8,128)S(1)} %get-tuple-element.27), channel_id=1, source_target_pairs={{8,0},{16,8},{24,16},{32,24},{40,32},{48,40},{56,48},{64,56},{72,6... | collective-permute-start | bytes 98312 | tf_op jit(solution)/shard_map/ppermute | solution.py:435
  (42 other events, 312.8 us)
Sparse Core Ops, SparseCore 0:
  23.5 61.5 all-gather.2
  93.7 46.3 all-gather.4
